TPU v7x, 32 devices: a whole 2x2x4 slice. The times are simulated.
32 devices in a mesh: section: 16 (over z, y, x), dp: 2 (over core).
Axes of the slice: x: 2, y: 2, z: 4, core: 2. Of those that a mesh axis runs over, the one named last changes fastest.
Arguments:
- pipe_maps: bfloat16 [16, 2, 8, 32, 384], P('section', 'dp'), may hold values from -6 to 6
- fresh_maps: bfloat16 [3, 2, 8, 32, 384], P(None, 'dp'), may hold values from -6 to 6
- teacher_weight: bfloat16 [32, 3, 3, 384, 384], P('section'), may hold values from -0.109375 to 0.109375
- student_depth: float32 [32, 49, 384], P('section'), may hold values from -0.875 to 0.875
- student_point: bfloat16 [32, 384, 384], P('section'), may hold values from -0.3125 to 0.3125
Outputs:
- final_maps: bfloat16 [16, 2, 8, 32, 384], P('section', 'dp')
- point_grad: float32 [32, 384, 384], P('section', None, 'dp')
- depth_grad: float32 [32, 49, 384], P('section', None, 'dp')
All inputs are finite; a program needn't handle non-finite values.
Results may differ from a plain program's by a relative error of at most 0.012.
Values may be sent and summed in bfloat16 or wider, within the bound.
A program may use at most 128 MiB of HBM per device.

v0:
```python
import functools

import jax
import jax.numpy as jnp
from jax import lax
from jax.experimental import pallas as pl
from jax.experimental.pallas import tpu as pltpu
from jax.sharding import PartitionSpec as P

LANES = 128
F32 = jnp.float32
BF16 = jnp.bfloat16
NT = (((1,), (1,)), ((), ()))


def gather_windows(vals, win_ref, width, height):
    chans = vals.shape[-1]
    rows = width * height
    h_of = lax.rem(lax.broadcasted_iota(jnp.int32, (rows, chans), 0), height)
    zero = jnp.zeros((height, chans), F32)
    cube = vals.reshape(width, height, chans)
    for row in range(3):
        dy = row - 1
        if dy:
            moved = pltpu.roll(cube, (-dy) % height, 1).reshape(rows, chans)
            moved = jnp.where((h_of + dy >= 0) & (h_of + dy < height), moved, 0.0)
        else:
            moved = vals
        for col in range(3):
            if col == 0:
                part = jnp.concatenate([zero, moved[: rows - height]], axis=0)
            elif col == 2:
                part = jnp.concatenate([moved[height:], zero], axis=0)
            else:
                part = moved
            tap = row * 3 + col
            win_ref[:, tap * chans : (tap + 1) * chans] = part.astype(BF16)


def teacher_kernel(width, height, lead_ref, fresh_ref, relay_ref, weight_ref, teach_ref, cur_ref, win_ref):
    lead = lead_ref[0] == 1
    current = jnp.where(lead, fresh_ref[...].astype(F32), relay_ref[...].astype(F32))
    cur_ref[...] = current.astype(BF16)
    gather_windows(current, win_ref, width, height)
    hidden = jnp.dot(win_ref[...], weight_ref[0], preferred_element_type=F32)
    gather_windows(jnp.maximum(hidden, 0.0), win_ref, width, height)
    second = jnp.dot(win_ref[...], weight_ref[1], preferred_element_type=F32)
    teach_ref[...] = (0.8 * (current + second)).astype(BF16)


def teacher(lead, fresh, relay, weight, width, height):
    rows, chans = fresh.shape
    vmem = pl.BlockSpec(memory_space=pltpu.VMEM)
    return pl.pallas_call(
        functools.partial(teacher_kernel, width, height),
        out_shape=(jax.ShapeDtypeStruct((rows, chans), BF16),) * 2,
        in_specs=[pl.BlockSpec(memory_space=pltpu.SMEM), vmem, vmem, vmem],
        out_specs=(vmem, vmem),
        scratch_shapes=[pltpu.VMEM((rows, 9 * chans), BF16)],
        compiler_params=pltpu.CompilerParams(vmem_limit_bytes=24 << 20),
        cost_estimate=pl.CostEstimate(
            flops=2 * 2 * 9 * rows * chans * chans, bytes_accessed=weight.size * 2, transcendentals=0
        ),
        name="teacher",
    )(lead, fresh, relay, weight)


def spread(cube, out_ref, block):
    width, height, _ = cube.shape
    h_of = lax.broadcasted_iota(jnp.int32, cube.shape, 1)
    for row in range(7):
        dy = row - 3
        moved = cube
        if dy:
            moved = pltpu.roll(cube, (-dy) % height, 1)
            moved = jnp.where((h_of + dy >= 0) & (h_of + dy < height), moved, 0.0)
        out_ref[block, row, 3 : 3 + width] = moved


def clear_edges(out_ref, width):
    edge = jnp.zeros(out_ref.shape[:2] + (3,) + out_ref.shape[3:], F32)
    out_ref[:, :, 0:3] = edge
    out_ref[:, :, 3 + width : 6 + width] = edge


def tap_sum(src_ref, block, taps_ref, which, start, count, flip):
    lanes = slice(block * LANES, (block + 1) * LANES)
    height = src_ref.shape[3]
    total = jnp.zeros((count, height, LANES), F32)
    for row in range(7):
        strip = src_ref[block, row, pl.ds(start, count + 6)]
        for col in range(7):
            tap = row * 7 + col
            tap = 48 - tap if flip else tap
            coef = jnp.broadcast_to(taps_ref[which, tap : tap + 1, lanes], (height, LANES))
            total = total + strip[col : col + count] * coef[None]
    return total


def gelu_pair(act):
    root = 0.7978845608028654
    square = act * act
    tanh = jnp.tanh(root * (act + 0.044715 * square * act))
    half = 0.5 * (1.0 + tanh)
    slope = half + 0.5 * act * (1.0 - tanh * tanh) * (root * (1.0 + 3.0 * 0.044715 * square))
    return act * half, slope


def student_kernel(
    width, height, step, cur_ref, teach_ref, taps_ref, point_ref,
    gel_ref, grad_ref, dk_ref, src0, src1, src2, slope0, slope1, dact, resid_ref,
):
    rows, chans = cur_ref.shape
    blocks = chans // LANES
    chunks = width // step
    srcs, slopes = (src0, src1), (slope0, slope1)
    area = width * height

    def lanes(block):
        return slice(block * LANES, (block + 1) * LANES)

    for ref in (src0, src1, src2):
        clear_edges(ref, width)
    for block in range(blocks):
        spread(cur_ref[:, lanes(block)].astype(F32).reshape(width, height, LANES), src0, block)

    def forward(which):
        def chunk(index, carry):
            start = index * step
            for block in range(blocks):
                act = tap_sum(srcs[which], block, taps_ref, which, start, step, False)
                gel, slope = gelu_pair(act)
                slopes[which][block, pl.ds(start, step)] = slope
                at = pl.ds(pl.multiple_of(start * height, step * height), step * height)
                gel_ref[which, at, lanes(block)] = gel.reshape(step * height, LANES).astype(BF16)
            return carry

        lax.fori_loop(0, chunks, chunk, 0)
        return jnp.dot(gel_ref[which], point_ref[which], preferred_element_type=F32)

    first = forward(0)
    for block in range(blocks):
        u_one = first[:, lanes(block)] + cur_ref[:, lanes(block)].astype(F32)
        spread(u_one.reshape(width, height, LANES), src1, block)
    second = forward(1)
    for block in range(blocks):
        u_one = src1[block, 3, 3 : 3 + width].reshape(rows, LANES)
        diff = u_one + second[:, lanes(block)] - teach_ref[:, lanes(block)].astype(F32)
        resid = diff * (4.0 / area)
        resid_ref[block] = resid.reshape(width, height, LANES)
        grad_ref[1, :, lanes(block)] = resid.astype(BF16)

    def taps_grad(which):
        def over_rows(row, carry):
            for block in range(blocks):
                sums = [jnp.zeros((height, LANES), F32)] * 7
                for index in range(chunks):
                    strip = srcs[which][block, row, pl.ds(index * step, step + 6)]
                    part = dact[block, pl.ds(index * step, step)]
                    for col in range(7):
                        sums[col] = sums[col] + jnp.sum(strip[col : col + step] * part, axis=0)
                for col in range(7):
                    dk_ref[which, block, row, col : col + 1, :] = jnp.sum(sums[col], axis=0, keepdims=True)
                dk_ref[which, block, row, 7:8, :] = jnp.zeros((1, LANES), F32)
            return carry

        lax.fori_loop(0, 7, over_rows, 0)

    def back_point(which):
        dgel = lax.dot_general(grad_ref[which], point_ref[which], NT, preferred_element_type=F32)
        for block in range(blocks):
            dact[block] = dgel[:, lanes(block)].reshape(width, height, LANES) * slopes[which][block]

    back_point(1)
    for block in range(blocks):
        spread(dact[block], src2, block)

    def chunk_back(index, carry):
        start = index * step
        for block in range(blocks):
            back = tap_sum(src2, block, taps_ref, 1, start, step, True)
            back = back + resid_ref[block, pl.ds(start, step)]
            at = pl.ds(pl.multiple_of(start * height, step * height), step * height)
            grad_ref[0, at, lanes(block)] = back.reshape(step * height, LANES).astype(BF16)
        return carry

    lax.fori_loop(0, chunks, chunk_back, 0)
    taps_grad(1)
    back_point(0)
    taps_grad(0)


def student(current, teach, taps, point, width, height):
    rows, chans = current.shape
    blocks = chans // LANES
    vmem = pl.BlockSpec(memory_space=pltpu.VMEM)
    spread_shape = pltpu.VMEM((blocks, 7, width + 6, height, LANES), F32)
    map_shape = pltpu.VMEM((blocks, width, height, LANES), F32)
    return pl.pallas_call(
        functools.partial(student_kernel, width, height, width // 2),
        out_shape=(
            jax.ShapeDtypeStruct((2, rows, chans), BF16),
            jax.ShapeDtypeStruct((2, rows, chans), BF16),
            jax.ShapeDtypeStruct((2, blocks, 7, 8, LANES), F32),
        ),
        in_specs=[vmem] * 4,
        out_specs=(vmem,) * 3,
        scratch_shapes=[spread_shape] * 3 + [map_shape] * 4,
        compiler_params=pltpu.CompilerParams(vmem_limit_bytes=32 << 20),
        cost_estimate=pl.CostEstimate(
            flops=10_000_000_000, bytes_accessed=8 * rows * chans, transcendentals=0
        ),
        name="student",
    )(current, teach, taps, point)


def body(pipe_maps, fresh_maps, teacher_weight, student_depth, student_point):
    _, _, height, width, chans = pipe_maps.shape
    rows = height * width
    blocks = chans // LANES
    lead = (lax.axis_index("section") == 0).astype(jnp.int32).reshape(1)
    sections = lax.axis_size("section")
    route = [(i, i + 1) for i in range(sections - 1)]

    def to_rows(maps):
        return jnp.swapaxes(maps, -3, -2).reshape(maps.shape[:-3] + (rows, chans))

    relay = to_rows(pipe_maps[0, 0])
    fresh = to_rows(fresh_maps[:, 0])
    weight = teacher_weight.reshape(2, 9 * chans, chans)
    ticks = fresh_maps.shape[0] + 1
    gels, grads, depth_total = [], [], None
    teach = relay
    for tick in range(ticks):
        mine = relay if tick == 0 else fresh[tick - 1]
        teach, current = teacher(lead, mine, relay, weight, width, height)
        if tick + 1 < ticks:
            relay = lax.ppermute(teach, "section", route)
        gel, grad, part = student(current, teach, student_depth, student_point, width, height)
        gels.append(gel)
        grads.append(grad)
        depth_total = part if depth_total is None else depth_total + part
    gel_all = jnp.concatenate(gels, axis=1)
    grad_all = jnp.concatenate(grads, axis=1)
    point_total = [
        lax.dot_general(grad_all[b], gel_all[b], (((0,), (0,)), ((), ())), preferred_element_type=F32)
        for b in range(2)
    ]
    depth_rows = depth_total[:, :, :, :7].transpose(1, 4, 0, 2, 3).reshape(chans, 98)
    packed = jnp.concatenate(point_total + [depth_rows], axis=1)
    parties = lax.axis_size("dp")
    share = chans // parties
    me = lax.axis_index("dp")
    total = lax.dynamic_slice_in_dim(packed, me * share, share, 0)
    for hop in range(1, parties):
        out = lax.dynamic_slice_in_dim(packed, lax.rem(me + hop, parties) * share, share, 0)
        pairs = [(i, (i + hop) % parties) for i in range(parties)]
        total = total + lax.ppermute(out.astype(BF16), "dp", pairs).astype(F32)
    point_grad = jnp.stack([total[:, b * chans : (b + 1) * chans].T for b in range(2)])
    depth_grad = total[:, 2 * chans :].T.reshape(2, 49, share)
    final = jnp.swapaxes(teach.reshape(width, height, chans), 0, 1)[None, None]
    return final, point_grad, depth_grad


def solution(mesh):
    placed = (
        P("section", "dp", None, None, None),
        P(None, "dp", None, None, None),
        P("section", None, None, None, None),
        P("section", None, None),
        P("section", None, None),
    )
    return jax.shard_map(
        body,
        mesh=mesh,
        in_specs=placed,
        out_specs=(
            P("section", "dp", None, None, None),
            P("section", None, "dp"),
            P("section", None, "dp"),
        ),
        check_vma=False,
    )
```

profile of v0, /device:TPU:0, one launch (start us, length us, event | category | flops | bytes accessed | tf_op | source)
XLA Modules:
  0.0 72.5 jit_solution(982787803351557119)
XLA Ops:
  0.6 1.0 %copy.38 = bf16[32,8,384]{2,1,0:T(8,128)(2,1)S(1)} copy(bf16[32,8,384]{2,0,1:T(8,128)(2,1)} %bitcast.72) | data formatting | bytes 393216 | tf_op jit(solution)/shard_map/transpose | solution.py:226
  1.6 0.0 copy-start
  1.6 2.5 %copy-done = bf16[2,3,3,384,384]{4,3,2,1,0:T(8,128)(2,1)S(1)} copy-done((bf16[2,3,3,384,384]{4,3,2,1,0:T(8,128)(2,1)S(1)}, bf16[2,3,3,384,384]{4,3,2,1,0:T(8,128)(2,1)}, u32[]{:S(2)}) %copy-start) | copy-done | bytes 5308440
  4.1 2.3 %teacher.4 = (bf16[256,384]{1,0:T(8,128)(2,1)S(1)}, bf16[256,384]{1,0:T(8,128)(2,1)S(1)}) custom-call(s32[1]{0:T(128)} %bitcast.lead_ref, bf16[256,384]{1,0:T(8,128)(2,1)S(1)} %bitcast.62, bf16[256,384]{1,0:T(8,128)(2,1)S(1)} %bitcast.63, bf16[2,3456,384]{2,1,0:T(8,128)(2,1)S(1)} %bitcast.56), custom_call_target="tpu_custom_call" | custom-call | flops 1358954496 | bytes 5308416 | tf_op jit(solution)/shard_map/teacher/pallas_call | solution.py:54
  6.5 0.0 copy-start.3
  6.5 0.0 copy-start.1
  6.5 5.0 %collective-permute-start = (bf16[256,384]{1,0:T(8,128)(2,1)S(1)}, bf16[256,384]{1,0:T(8,128)(2,1)S(1)}, u32[]{:S(2)}, u32[]{:S(2)}) collective-permute-start(bf16[256,384]{1,0:T(8,128)(2,1)S(1)} %get-tuple-element.23.teach_ref), channel_id=1, source_target_pairs={{0,2},{2,4},{4,6},{6,8},{8,10},{10,12},{12,14},{14,16},{16,18},{18... | collective-permute-start | bytes 589832 | tf_op jit(solution)/shard_map/ppermute | solution.py:238
  11.5 0.0 copy-done.2
  11.5 0.1 fusion.3
  11.6 0.1 copy.41
  11.7 0.1 copy.40
  11.7 0.0 slice-start
  11.8 0.1 copy.39
  11.8 0.0 copy-done.3
  11.9 0.0 copy-done.1
  11.9 0.0 slice-start.1
  11.9 10.0 %student.4 = (bf16[2,256,384]{2,1,0:T(8,128)(2,1)S(1)}, bf16[2,256,384]{2,1,0:T(8,128)(2,1)S(1)}, f32[2,3,7,8,128]{4,3,2,1,0:T(8,128)S(1)}) custom-call(bf16[256,384]{1,0:T(8,128)(2,1)S(1)} %get-tuple-element.27.cur_ref, bf16[256,384]{1,0:T(8,128)(2,1)S(1)} %get-tuple-element.23.teach_ref, f32[2,49,384]{2,1,0:T(8,128)S(1)} %copy.24.taps_ref, ...), custom_call_target="tpu_custom_call" | custom-call | flops 10000000000 | bytes 786432 | tf_op jit(solution)/shard_map/student/pallas_call | solution.py:199
  22.0 0.0 collective-permute-done.relay_ref
  22.0 0.0 slice-done
  22.0 0.0 slice-done.1
  22.0 2.3 %teacher.5 = (bf16[256,384]{1,0:T(8,128)(2,1)S(1)}, bf16[256,384]{1,0:T(8,128)(2,1)S(1)}) custom-call(s32[1]{0:T(128)} %bitcast.lead_ref, bf16[256,384]{1,0:T(8,128)(2,1)S(1)} %bitcast.66, bf16[256,384]{1,0:T(8,128)(2,1)S(1)} %collective-permute-done.relay_ref, bf16[2,3456,384]{2,1,0:T(8,128)(2,1)S(1)} %bitcast.59), custom_call_target="tpu_custom_call" | custom-call | flops 1358954496 | bytes 5308416 | tf_op jit(solution)/shard_map/teacher/pallas_call | solution.py:54
  24.3 3.6 %collective-permute-start.1 = (bf16[256,384]{1,0:T(8,128)(2,1)S(1)}, bf16[256,384]{1,0:T(8,128)(2,1)S(1)}, u32[]{:S(2)}, u32[]{:S(2)}) collective-permute-start(bf16[256,384]{1,0:T(8,128)(2,1)S(1)} %get-tuple-element.24.teach_ref), channel_id=1, source_target_pairs={{0,2},{2,4},{4,6},{6,8},{8,10},{10,12},{12,14},{14,16},{16,18},{18... | collective-permute-start | bytes 589832 | tf_op jit(solution)/shard_map/ppermute | solution.py:238
  27.9 10.0 %student.5 = (bf16[2,256,384]{2,1,0:T(8,128)(2,1)S(1)}, bf16[2,256,384]{2,1,0:T(8,128)(2,1)S(1)}, f32[2,3,7,8,128]{4,3,2,1,0:T(8,128)S(1)}) custom-call(bf16[256,384]{1,0:T(8,128)(2,1)S(1)} %get-tuple-element.29.cur_ref, bf16[256,384]{1,0:T(8,128)(2,1)S(1)} %get-tuple-element.24.teach_ref, f32[2,49,384]{2,1,0:T(8,128)S(1)} %copy.24.taps_ref, ...), custom_call_target="tpu_custom_call" | custom-call | flops 10000000000 | bytes 786432 | tf_op jit(solution)/shard_map/student/pallas_call | solution.py:199
  37.8 0.1 constant_dynamic-update-slice_fusion.2
  37.9 0.1 constant_dynamic-update-slice_fusion.6
  38.0 0.0 collective-permute-done.1.relay_ref
  38.0 2.3 %teacher.6 = (bf16[256,384]{1,0:T(8,128)(2,1)S(1)}, bf16[256,384]{1,0:T(8,128)(2,1)S(1)}) custom-call(s32[1]{0:T(128)} %bitcast.lead_ref, bf16[256,384]{1,0:T(8,128)(2,1)S(1)} %bitcast.65, bf16[256,384]{1,0:T(8,128)(2,1)S(1)} %collective-permute-done.1.relay_ref, bf16[2,3456,384]{2,1,0:T(8,128)(2,1)S(1)} %bitcast.60), custom_call_target="tpu_custom_call" | custom-call | flops 1358954496 | bytes 5308416 | tf_op jit(solution)/shard_map/teacher/pallas_call | solution.py:54
  40.2 3.6 %collective-permute-start.2 = (bf16[256,384]{1,0:T(8,128)(2,1)S(1)}, bf16[256,384]{1,0:T(8,128)(2,1)S(1)}, u32[]{:S(2)}, u32[]{:S(2)}) collective-permute-start(bf16[256,384]{1,0:T(8,128)(2,1)S(1)} %get-tuple-element.25.teach_ref), channel_id=1, source_target_pairs={{0,2},{2,4},{4,6},{6,8},{8,10},{10,12},{12,14},{14,16},{16,18},{18... | collective-permute-start | bytes 589832 | tf_op jit(solution)/shard_map/ppermute | solution.py:238
  43.9 10.0 %student.6 = (bf16[2,256,384]{2,1,0:T(8,128)(2,1)S(1)}, bf16[2,256,384]{2,1,0:T(8,128)(2,1)S(1)}, f32[2,3,7,8,128]{4,3,2,1,0:T(8,128)S(1)}) custom-call(bf16[256,384]{1,0:T(8,128)(2,1)S(1)} %get-tuple-element.31.cur_ref, bf16[256,384]{1,0:T(8,128)(2,1)S(1)} %get-tuple-element.25.teach_ref, f32[2,49,384]{2,1,0:T(8,128)S(1)} %copy.24.taps_ref, ...), custom_call_target="tpu_custom_call" | custom-call | flops 10000000000 | bytes 786432 | tf_op jit(solution)/shard_map/student/pallas_call | solution.py:199
  53.9 0.1 constant_dynamic-update-slice_fusion.1
  53.9 0.1 constant_dynamic-update-slice_fusion.5
  54.0 0.0 collective-permute-done.2.relay_ref
  54.0 2.3 %teacher.7 = (bf16[256,384]{1,0:T(8,128)(2,1)S(1)}, bf16[256,384]{1,0:T(8,128)(2,1)S(1)}) custom-call(s32[1]{0:T(128)} %bitcast.lead_ref, bf16[256,384]{1,0:T(8,128)(2,1)S(1)} %bitcast.64, bf16[256,384]{1,0:T(8,128)(2,1)S(1)} %collective-permute-done.2.relay_ref, bf16[2,3456,384]{2,1,0:T(8,128)(2,1)S(1)} %bitcast.61), custom_call_target="tpu_custom_call" | custom-call | flops 1358954496 | bytes 5308416 | tf_op jit(solution)/shard_map/teacher/pallas_call | solution.py:54
  56.3 10.2 %student.7 = (bf16[2,256,384]{2,1,0:T(8,128)(2,1)S(1)}, bf16[2,256,384]{2,1,0:T(8,128)(2,1)S(1)}, f32[2,3,7,8,128]{4,3,2,1,0:T(8,128)S(1)}) custom-call(bf16[256,384]{1,0:T(8,128)(2,1)S(1)} %get-tuple-element.33.cur_ref, bf16[256,384]{1,0:T(8,128)(2,1)S(1)} %get-tuple-element.26.teach_ref, f32[2,49,384]{2,1,0:T(8,128)S(1)} %copy.24.taps_ref, ...), custom_call_target="tpu_custom_call" | custom-call | flops 10000000000 | bytes 786432 | tf_op jit(solution)/shard_map/student/pallas_call | solution.py:199
  66.5 0.2 constant_dynamic-update-slice_fusion
  66.7 0.6 fusion
  67.3 0.6 fusion.1
  68.0 0.1 copy.28
  68.1 0.1 pad_maximum_fusion
  68.2 0.2 dynamic-slice_convert_fusion
  68.4 0.1 collective-permute-start.3
  68.5 0.7 copy.37
  69.2 1.1 %collective-permute-done.3 = bf16[192,866]{0,1:T(8,128)(2,1)S(1)} collective-permute-done((bf16[192,866]{0,1:T(8,128)(2,1)S(1)}, bf16[192,866]{0,1:T(8,128)(2,1)S(1)}, u32[]{:S(2)}, u32[]{:S(2)}) %collective-permute-start.3) | collective-permute-done | bytes 332576 | tf_op jit(solution)/shard_map/ppermute | solution.py:258
  70.3 0.3 convert_add_fusion
  70.6 0.1 slice_bitcast_fusion.9
  70.6 0.1 pad_maximum_fusion.1
  70.7 1.1 %copy.29 = f32[2,384,192]{1,2,0:T(8,128)} copy(f32[2,384,192]{2,1,0:T(8,128)S(1)} %pad_maximum_fusion.1) | data formatting | bytes 1179648
  71.8 0.7 copy.30
  (10 shorter events, 0.2 us)
Async XLA Ops:
  1.6 2.5 %copy-start = (bf16[2,3,3,384,384]{4,3,2,1,0:T(8,128)(2,1)S(1)}, bf16[2,3,3,384,384]{4,3,2,1,0:T(8,128)(2,1)}, u32[]{:S(2)}) copy-start(bf16[2,3,3,384,384]{4,3,2,1,0:T(8,128)(2,1)} %param.7) | copy-start | bytes 15925252
  4.1 7.4 %copy-start.2 = (bf16[3,1,8,32,384]{4,3,2,1,0:T(8,128)(2,1)S(1)}, bf16[3,1,8,32,384]{4,3,2,1,0:T(8,128)(2,1)}, u32[]{:S(2)}) copy-start(bf16[3,1,8,32,384]{4,3,2,1,0:T(8,128)(2,1)} %param.6) | copy-start | bytes 1769476
  6.5 5.4 %copy-start.3 = (f32[2,49,384]{2,0,1:T(2,128)S(1)}, f32[2,49,384]{2,0,1:T(2,128)}, u32[]{:S(2)}) copy-start(f32[2,49,384]{2,0,1:T(2,128)} %param.8) | copy-start | bytes 451588
  6.5 5.4 %copy-start.1 = (bf16[2,384,384]{2,1,0:T(8,128)(2,1)S(1)}, bf16[2,384,384]{2,1,0:T(8,128)(2,1)}, u32[]{:S(2)}) copy-start(bf16[2,384,384]{2,1,0:T(8,128)(2,1)} %point_ref.7) | copy-start | bytes 1769476
  6.5 15.5 %collective-permute-start = (bf16[256,384]{1,0:T(8,128)(2,1)S(1)}, bf16[256,384]{1,0:T(8,128)(2,1)S(1)}, u32[]{:S(2)}, u32[]{:S(2)}) collective-permute-start(bf16[256,384]{1,0:T(8,128)(2,1)S(1)} %get-tuple-element.23.teach_ref), channel_id=1, source_target_pairs={{0,2},{2,4},{4,6},{6,8},{8,10},{10,12},{12,14},{14,16},{16,18},{18... | collective-permute-start | bytes 589832 | tf_op jit(solution)/shard_map/ppermute | solution.py:238
  11.7 10.2 %slice-start = ((s8[5308416]{0:T(1024)(128)(4,1)}), s8[1114112]{0:T(1024)(128)(4,1)S(1)}, s32[]{:S(2)}) async-start(s8[5308416]{0:T(1024)(128)(4,1)} %bitcast.57), calls=%async_computation | async-start | bytes 2228224
  11.9 10.1 %slice-start.1 = ((s8[5308416]{0:T(1024)(128)(4,1)}), s8[4194304]{0:T(1024)(128)(4,1)S(1)}, s32[]{:S(2)}) async-start(s8[5308416]{0:T(1024)(128)(4,1)} %bitcast.57), calls=%async_computation.1 | async-start | bytes 8388608
  24.3 13.7 %collective-permute-start.1 = (bf16[256,384]{1,0:T(8,128)(2,1)S(1)}, bf16[256,384]{1,0:T(8,128)(2,1)S(1)}, u32[]{:S(2)}, u32[]{:S(2)}) collective-permute-start(bf16[256,384]{1,0:T(8,128)(2,1)S(1)} %get-tuple-element.24.teach_ref), channel_id=1, source_target_pairs={{0,2},{2,4},{4,6},{6,8},{8,10},{10,12},{12,14},{14,16},{16,18},{18... | collective-permute-start | bytes 589832 | tf_op jit(solution)/shard_map/ppermute | solution.py:238
  40.2 13.8 %collective-permute-start.2 = (bf16[256,384]{1,0:T(8,128)(2,1)S(1)}, bf16[256,384]{1,0:T(8,128)(2,1)S(1)}, u32[]{:S(2)}, u32[]{:S(2)}) collective-permute-start(bf16[256,384]{1,0:T(8,128)(2,1)S(1)} %get-tuple-element.25.teach_ref), channel_id=1, source_target_pairs={{0,2},{2,4},{4,6},{6,8},{8,10},{10,12},{12,14},{14,16},{16,18},{18... | collective-permute-start | bytes 589832 | tf_op jit(solution)/shard_map/ppermute | solution.py:238
  68.4 1.9 %collective-permute-start.3 = (bf16[192,866]{0,1:T(8,128)(2,1)S(1)}, bf16[192,866]{0,1:T(8,128)(2,1)S(1)}, u32[]{:S(2)}, u32[]{:S(2)}) collective-permute-start(bf16[192,866]{0,1:T(8,128)(2,1)S(1)} %dynamic-slice_convert_fusion), channel_id=1, source_target_pairs={{0,1},{1,0},{2,3},{3,2},{4,5},{5,4},{6,7},{7,6},{8,9},{9,8},{10,11... | collective-permute-start | bytes 997640 | tf_op jit(solution)/shard_map/ppermute | solution.py:258
where the time goes:
time: 72.7 us; the launch traced here: 72.5 us
  Pallas kernels  49.2 us (68%)
  starting transfers between devices  12.3 us (17%)
  local copies, waits for them, and re-layouts  7.13 us (10%)
  matrix products  1.23 us (2%)
  waiting for transfers between devices  1.09 us (1%)
  between operations  1.01 us (1%)
    pallas_call x4, Pallas kernels, student(): pl.pallas_call(functools.partial(student_kernel, width, height, width //...  40.1 us
    ppermute x3, starting transfers between devices, body(): relay = lax.ppermute(teach, 'section', route)  12.2 us
    pallas_call x4, Pallas kernels, teacher(): pl.pallas_call(functools.partial(teacher_kernel, width, height), out_shap...  9.1 us
    unnamed x23, local copies, waits for them, and re-layouts  4.7 us
  transfers between devices with their start and end apart: 4, of which 1 were waited for; matrix products, arithmetic and copies ran while one was open for 2% of the time, Pallas kernels for 41%

commit v1 on v0

v1 whole, which is shorter than its diff:
```python
import functools

import jax
import jax.numpy as jnp
from jax import lax
from jax.experimental import pallas as pl
from jax.experimental.pallas import tpu as pltpu
from jax.sharding import PartitionSpec as P

LANES = 128
F32 = jnp.float32
BF16 = jnp.bfloat16
NT = (((1,), (1,)), ((), ()))


def gather_windows(vals, win_ref, height):
    rows, chans = vals.shape
    pair = 2 * height
    h_of = lax.rem(lax.broadcasted_iota(jnp.int32, (rows, chans), 0), height)
    zero = jnp.zeros((height, chans), F32)
    cube = vals.reshape(rows // height, height, chans)
    for row in range(3):
        dy = row - 1
        moved = vals
        if dy:
            moved = pltpu.roll(cube, (-dy) % height, 1).reshape(rows, chans)
            moved = jnp.where((h_of + dy >= 0) & (h_of + dy < height), moved, 0.0)
        for col in range(3):
            if col == 0:
                part = jnp.concatenate([zero, moved[rows - pair : rows - height], moved[: rows - pair]], axis=0)
            elif col == 2:
                part = jnp.concatenate([moved[pair:], moved[height:pair], zero], axis=0)
            else:
                part = moved
            tap = row * 3 + col
            win_ref[:, tap * chans : (tap + 1) * chans] = part.astype(BF16)


def teacher_kernel(height, lead_ref, fresh_ref, relay_ref, weight_ref, teach_ref, cur_ref, win_ref):
    lead = lead_ref[0] == 1
    current = jnp.where(lead, fresh_ref[...].astype(F32), relay_ref[...].astype(F32))
    cur_ref[...] = current.astype(BF16)
    gather_windows(current, win_ref, height)
    hidden = jnp.dot(win_ref[...], weight_ref[0], preferred_element_type=F32)
    gather_windows(jnp.maximum(hidden, 0.0), win_ref, height)
    second = jnp.dot(win_ref[...], weight_ref[1], preferred_element_type=F32)
    teach_ref[...] = (0.8 * (current + second)).astype(BF16)


def teacher(lead, fresh, relay, weight, height):
    rows, chans = fresh.shape
    vmem = pl.BlockSpec(memory_space=pltpu.VMEM)
    return pl.pallas_call(
        functools.partial(teacher_kernel, height),
        out_shape=(jax.ShapeDtypeStruct((rows, chans), BF16),) * 2,
        in_specs=[pl.BlockSpec(memory_space=pltpu.SMEM), vmem, vmem, vmem],
        out_specs=(vmem, vmem),
        scratch_shapes=[pltpu.VMEM((rows, 9 * chans), BF16)],
        compiler_params=pltpu.CompilerParams(vmem_limit_bytes=24 << 20),
        cost_estimate=pl.CostEstimate(
            flops=2 * 2 * 9 * rows * chans * chans, bytes_accessed=weight.size * 2, transcendentals=0
        ),
        name="teacher",
    )(lead, fresh, relay, weight)


def spread(vals, out_ref, block, height):
    pair = vals.reshape(-1, 2 * height, LANES)
    low, high = pair[:, :height], pair[:, height:]
    h_of = lax.broadcasted_iota(jnp.int32, low.shape, 1)
    zero = jnp.zeros((3, height, LANES), F32)
    for row in range(7):
        dy = row - 3
        one, two = low, high
        if dy:
            keep = (h_of + dy >= 0) & (h_of + dy < height)
            one = jnp.where(keep, pltpu.roll(low, (-dy) % height, 1), 0.0)
            two = jnp.where(keep, pltpu.roll(high, (-dy) % height, 1), 0.0)
        left = jnp.concatenate([zero, one, two[:3]], axis=0)
        right = jnp.concatenate([one[-3:], two, zero], axis=0)
        out_ref[block, row] = jnp.concatenate([left, right], axis=1).astype(BF16)


def tap_sum(src_ref, block, taps_ref, which, start, count, flip):
    total, held = None, None
    for row in range(7):
        strip = src_ref[block, row, pl.ds(start, count + 6)]
        terms = []
        for col in range(7):
            tap = row * 7 + col
            tap = 48 - tap if flip else tap
            terms.append(strip[col : col + count] * taps_ref[which, block, tap][None])
        while len(terms) > 1:
            terms = [sum(terms[i + 1 : i + 2], terms[i]) for i in range(0, len(terms), 2)]
        if held is None and row < 6:
            held = terms[0]
            continue
        part = terms[0] if held is None else held + terms[0]
        held = None
        total = part.astype(F32) if total is None else total + part.astype(F32)
    return total


def gelu_pair(act):
    root = 0.7978845608028654
    square = act * act
    tanh = jnp.tanh(root * (act + 0.044715 * square * act))
    half = 0.5 * (1.0 + tanh)
    slope = half + 0.5 * act * (1.0 - tanh * tanh) * (root * (1.0 + 3.0 * 0.044715 * square))
    return act * half, slope


def student_kernel(
    height, step, cur_ref, teach_ref, taps_ref, point_ref,
    gel_ref, grad_ref, dk_ref, src0, src1, src2, slope0, slope1, dact, u_one_ref, resid_ref,
):
    rows, chans = cur_ref.shape
    blocks = chans // LANES
    pair = 2 * height
    chunks = rows // (pair * step)
    srcs, slopes = (src0, src1), (slope0, slope1)

    def lanes(block):
        return slice(block * LANES, (block + 1) * LANES)

    def span(index):
        return pl.ds(pl.multiple_of(index * step * pair, step * pair), step * pair)

    for block in range(blocks):
        spread(cur_ref[:, lanes(block)].astype(F32), src0, block, height)

    def forward(which):
        def chunk(index, carry):
            for block in range(blocks):
                act = tap_sum(srcs[which], block, taps_ref, which, index * step, step, False)
                gel, slope = gelu_pair(act.reshape(step * pair, LANES))
                slopes[which][span(index), lanes(block)] = slope
                gel_ref[which, span(index), lanes(block)] = gel.astype(BF16)
            return carry

        lax.fori_loop(0, chunks, chunk, 0)
        return jnp.dot(gel_ref[which], point_ref[which], preferred_element_type=F32)

    u_one_ref[...] = forward(0) + cur_ref[...].astype(F32)
    for block in range(blocks):
        spread(u_one_ref[:, lanes(block)], src1, block, height)
    diff = forward(1) + u_one_ref[...] - teach_ref[...].astype(F32)
    resid = diff * (4.0 / rows)
    resid_ref[...] = resid
    grad_ref[1] = resid.astype(BF16)

    def taps_grad(which):
        def over_rows(row, carry):
            for block in range(blocks):
                strip = srcs[which][block, row]
                part = dact[:, lanes(block)].reshape(-1, pair, LANES)
                count = part.shape[0]
                for col in range(7):
                    prod = strip[col : col + count] * part
                    size = count
                    while size > 1:
                        size //= 2
                        prod = prod[:size] + prod[size:]
                    line = jnp.sum(prod[0].astype(F32), axis=0, keepdims=True)
                    dk_ref[which, block, row, col : col + 1, :] = line
                dk_ref[which, block, row, 7:8, :] = jnp.zeros((1, LANES), F32)
            return carry

        lax.fori_loop(0, 7, over_rows, 0)

    def back_point(which):
        dgel = lax.dot_general(grad_ref[which], point_ref[which], NT, preferred_element_type=F32)
        return dgel * slopes[which][...]

    dact_one = back_point(1)
    dact[...] = dact_one.astype(BF16)
    for block in range(blocks):
        spread(dact_one[:, lanes(block)], src2, block, height)

    def chunk_back(index, carry):
        for block in range(blocks):
            back = tap_sum(src2, block, taps_ref, 1, index * step, step, True)
            back = back.reshape(step * pair, LANES) + resid_ref[span(index), lanes(block)]
            grad_ref[0, span(index), lanes(block)] = back.astype(BF16)
        return carry

    lax.fori_loop(0, chunks, chunk_back, 0)
    taps_grad(1)
    dact[...] = back_point(0).astype(BF16)
    taps_grad(0)


def student(current, teach, taps, point, height):
    rows, chans = current.shape
    blocks = chans // LANES
    half = rows // (2 * height)
    vmem = pl.BlockSpec(memory_space=pltpu.VMEM)
    spread_shape = pltpu.VMEM((blocks, 7, half + 6, 2 * height, LANES), BF16)
    map_shape = pltpu.VMEM((rows, chans), F32)
    return pl.pallas_call(
        functools.partial(student_kernel, height, half // 2),
        out_shape=(
            jax.ShapeDtypeStruct((2, rows, chans), BF16),
            jax.ShapeDtypeStruct((2, rows, chans), BF16),
            jax.ShapeDtypeStruct((2, blocks, 7, 8, LANES), F32),
        ),
        in_specs=[vmem] * 4,
        out_specs=(vmem,) * 3,
        scratch_shapes=[spread_shape] * 3
        + [map_shape] * 2
        + [pltpu.VMEM((rows, chans), BF16)]
        + [map_shape] * 2,
        compiler_params=pltpu.CompilerParams(vmem_limit_bytes=32 << 20),
        cost_estimate=pl.CostEstimate(
            flops=10_000_000_000, bytes_accessed=8 * rows * chans, transcendentals=0
        ),
        name="student",
    )(current, teach, taps, point)


def body(pipe_maps, fresh_maps, teacher_weight, student_depth, student_point):
    _, _, height, width, chans = pipe_maps.shape
    rows = height * width
    blocks = chans // LANES
    lead = (lax.axis_index("section") == 0).astype(jnp.int32).reshape(1)
    sections = lax.axis_size("section")
    route = [(i, i + 1) for i in range(sections - 1)]

    def to_rows(maps):
        front = maps.shape[:-3]
        split = maps.reshape(front + (height, 2, width // 2, chans))
        return jnp.swapaxes(split, -4, -2).reshape(front + (rows, chans))

    relay = to_rows(pipe_maps[0, 0])
    fresh = to_rows(fresh_maps[:, 0])
    weight = teacher_weight.reshape(2, 9 * chans, chans)
    taps = student_depth.astype(BF16).reshape(2, -1, blocks, 1, LANES).swapaxes(1, 2)
    taps = jnp.broadcast_to(taps, taps.shape[:3] + (2 * height, LANES))
    ticks = fresh_maps.shape[0] + 1
    gels, grads, depth_total = [], [], None
    teach = relay
    for tick in range(ticks):
        mine = relay if tick == 0 else fresh[tick - 1]
        teach, current = teacher(lead, mine, relay, weight, height)
        if tick + 1 < ticks:
            relay = lax.ppermute(teach, "section", route)
        gel, grad, part = student(current, teach, taps, student_point, height)
        gels.append(gel)
        grads.append(grad)
        depth_total = part if depth_total is None else depth_total + part
    gel_all = jnp.concatenate(gels, axis=1)
    grad_all = jnp.concatenate(grads, axis=1)
    point_total = [
        lax.dot_general(grad_all[b], gel_all[b], (((0,), (0,)), ((), ())), preferred_element_type=F32)
        for b in range(2)
    ]
    depth_rows = depth_total[:, :, :, :7].transpose(1, 4, 0, 2, 3).reshape(chans, 98)
    packed = jnp.concatenate(point_total + [depth_rows], axis=1)
    parties = lax.axis_size("dp")
    share = chans // parties
    me = lax.axis_index("dp")
    total = lax.dynamic_slice_in_dim(packed, me * share, share, 0)
    for hop in range(1, parties):
        out = lax.dynamic_slice_in_dim(packed, lax.rem(me + hop, parties) * share, share, 0)
        pairs = [(i, (i + hop) % parties) for i in range(parties)]
        total = total + lax.ppermute(out.astype(BF16), "dp", pairs).astype(F32)
    point_grad = jnp.stack([total[:, b * chans : (b + 1) * chans].T for b in range(2)])
    depth_grad = total[:, 2 * chans :].T.reshape(2, 49, share)
    final = jnp.swapaxes(teach.reshape(width // 2, 2, height, chans), 0, 2)
    final = final.reshape(1, 1, height, width, chans)
    return final, point_grad, depth_grad


def solution(mesh):
    placed = (
        P("section", "dp", None, None, None),
        P(None, "dp", None, None, None),
        P("section", None, None, None, None),
        P("section", None, None),
        P("section", None, None),
    )
    return jax.shard_map(
        body,
        mesh=mesh,
        in_specs=placed,
        out_specs=(
            P("section", "dp", None, None, None),
            P("section", None, "dp"),
            P("section", None, "dp"),
        ),
        check_vma=False,
    )
```

time: 72.7 us -> 81.6 us (1.12)
  Pallas kernels: 49.2 us -> 53.8 us
  local copies, waits for them, and re-layouts: 7.13 us -> 11.4 us
    pallas_call x8, Pallas kernels: 49.2 us -> 53.8 us  [the longest x4 44.4 us: student(): pl.pallas_call(functools.partial(student_kernel, height, half // 2), out_...]
    unnamed x23 -> x28, local copies, waits for them, and re-layouts: 4.7 us -> 8.7 us
    another operation x0 -> x2, local copies, waits for them, and re-layouts: none -> 1.19 us  [to_rows(): split = maps.reshape(front + (height, 2, width // 2, chans))]
  transfers between devices with their start and end apart: 4 -> 4, of which waited for: 1 -> 1; matrix products, arithmetic and copies ran while one was open for 2% -> 4% of each run, Pallas kernels for 41% -> 41%
where the time goes in v1:
time: 81.6 us; the launch traced here: 81.4 us
  Pallas kernels  53.8 us (66%)
  starting transfers between devices  12.3 us (15%)
  local copies, waits for them, and re-layouts  11.4 us (14%)
  matrix products  1.23 us (2%)
  waiting for transfers between devices  1.07 us (1%)
  between operations  1.01 us (1%)
    pallas_call x4, Pallas kernels, student(): pl.pallas_call(functools.partial(student_kernel, height, half // 2), out_...  44.4 us
    ppermute x3, starting transfers between devices, body(): relay = lax.ppermute(teach, 'section', route)  12.2 us
    pallas_call x4, Pallas kernels, teacher(): pl.pallas_call(functools.partial(teacher_kernel, height), out_shape=(jax....  9.37 us
    unnamed x28, local copies, waits for them, and re-layouts  8.7 us
  transfers between devices with their start and end apart: 4, of which 1 were waited for; matrix products, arithmetic and copies ran while one was open for 4% of the time, Pallas kernels for 41%

profile of v1, /device:TPU:0, one launch (start us, length us, event | category | flops | bytes accessed | tf_op | source)
XLA Modules:
  0.0 81.4 jit_solution(899125050867635520)
XLA Ops:
  0.6 1.0 %copy.15 = bf16[8,2,16,384]{3,0,1,2:T(8,128)(2,1)S(1)} copy(bf16[8,2,16,384]{3,2,1,0:T(8,128)(2,1)} %bitcast.70) | data formatting | bytes 393216 | tf_op jit(solution)/shard_map/reshape;squeeze | solution.py:231
  1.6 0.0 copy-start
  1.6 2.5 %copy-done = bf16[2,3,3,384,384]{4,3,2,1,0:T(8,128)(2,1)S(1)} copy-done((bf16[2,3,3,384,384]{4,3,2,1,0:T(8,128)(2,1)S(1)}, bf16[2,3,3,384,384]{4,3,2,1,0:T(8,128)(2,1)}, u32[]{:S(2)}) %copy-start) | copy-done | bytes 5308440
  4.1 2.4 %teacher.4 = (bf16[256,384]{1,0:T(8,128)(2,1)S(1)}, bf16[256,384]{1,0:T(8,128)(2,1)S(1)}) custom-call(s32[1]{0:T(128)} %bitcast.lead_ref, bf16[256,384]{1,0:T(8,128)(2,1)S(1)} %bitcast.58, bf16[256,384]{1,0:T(8,128)(2,1)S(1)} %bitcast.59, bf16[2,3456,384]{2,1,0:T(8,128)(2,1)S(1)} %bitcast.52), custom_call_target="tpu_custom_call" | custom-call | flops 1358954496 | bytes 5308416 | tf_op jit(solution)/shard_map/teacher/pallas_call | solution.py:53
  6.5 0.0 copy-start.2
  6.5 5.0 %collective-permute-start = (bf16[256,384]{1,0:T(8,128)(2,1)S(1)}, bf16[256,384]{1,0:T(8,128)(2,1)S(1)}, u32[]{:S(2)}, u32[]{:S(2)}) collective-permute-start(bf16[256,384]{1,0:T(8,128)(2,1)S(1)} %get-tuple-element.23.teach_ref), channel_id=1, source_target_pairs={{0,2},{2,4},{4,6},{6,8},{8,10},{10,12},{12,14},{14,16},{16,18},{18... | collective-permute-start | bytes 589832 | tf_op jit(solution)/shard_map/ppermute | solution.py:246
  11.6 0.0 copy-done.3
  11.6 0.2 copy.23
  11.8 0.0 copy-done.4
  11.8 0.1 convert_element_type.10
  11.9 0.1 reshape.45
  12.0 0.2 broadcast_in_dim.8.taps_ref
  12.2 11.0 %student.4 = (bf16[2,256,384]{2,1,0:T(8,128)(2,1)S(1)}, bf16[2,256,384]{2,1,0:T(8,128)(2,1)S(1)}, f32[2,3,7,8,128]{4,3,2,1,0:T(8,128)S(1)}) custom-call(bf16[256,384]{1,0:T(8,128)(2,1)S(1)} %get-tuple-element.27.cur_ref, bf16[256,384]{1,0:T(8,128)(2,1)S(1)} %get-tuple-element.23.teach_ref, bf16[2,3,49,16,128]{4,3,2,1,0:T(8,128)(2,1)S(1)} %broadcast_in_dim.8.taps_ref, ...), custom_call_target="tpu_custom_call" | custom-call | flops 10000000000 | bytes 786432 | tf_op jit(solution)/shard_map/student/pallas_call | solution.py:200
  23.2 0.8 constant_dynamic-update-slice_fusion.3
  24.0 0.8 constant_dynamic-update-slice_fusion.7
  24.8 0.1 fusion.3
  24.9 0.0 collective-permute-done.relay_ref
  24.9 0.0 copy-start.1
  24.9 2.5 %copy-done.1 = bf16[2,3,3,384,384]{4,3,2,1,0:T(8,128)(2,1)S(1)} copy-done((bf16[2,3,3,384,384]{4,3,2,1,0:T(8,128)(2,1)S(1)}, bf16[2,3,3,384,384]{4,3,2,1,0:T(8,128)(2,1)}, u32[]{:S(2)}) %copy-start.1) | copy-done | bytes 5308440
  27.4 2.4 %teacher.5 = (bf16[256,384]{1,0:T(8,128)(2,1)S(1)}, bf16[256,384]{1,0:T(8,128)(2,1)S(1)}) custom-call(s32[1]{0:T(128)} %bitcast.lead_ref, bf16[256,384]{1,0:T(8,128)(2,1)S(1)} %bitcast.62, bf16[256,384]{1,0:T(8,128)(2,1)S(1)} %collective-permute-done.relay_ref, bf16[2,3456,384]{2,1,0:T(8,128)(2,1)S(1)} %bitcast.53), custom_call_target="tpu_custom_call" | custom-call | flops 1358954496 | bytes 5308416 | tf_op jit(solution)/shard_map/teacher/pallas_call | solution.py:53
  29.8 3.6 %collective-permute-start.1 = (bf16[256,384]{1,0:T(8,128)(2,1)S(1)}, bf16[256,384]{1,0:T(8,128)(2,1)S(1)}, u32[]{:S(2)}, u32[]{:S(2)}) collective-permute-start(bf16[256,384]{1,0:T(8,128)(2,1)S(1)} %get-tuple-element.24.teach_ref), channel_id=1, source_target_pairs={{0,2},{2,4},{4,6},{6,8},{8,10},{10,12},{12,14},{14,16},{16,18},{18... | collective-permute-start | bytes 589832 | tf_op jit(solution)/shard_map/ppermute | solution.py:246
  33.4 0.0 slice-start.1
  33.4 11.0 %student.5 = (bf16[2,256,384]{2,1,0:T(8,128)(2,1)S(1)}, bf16[2,256,384]{2,1,0:T(8,128)(2,1)S(1)}, f32[2,3,7,8,128]{4,3,2,1,0:T(8,128)S(1)}) custom-call(bf16[256,384]{1,0:T(8,128)(2,1)S(1)} %get-tuple-element.29.cur_ref, bf16[256,384]{1,0:T(8,128)(2,1)S(1)} %get-tuple-element.24.teach_ref, bf16[2,3,49,16,128]{4,3,2,1,0:T(8,128)(2,1)S(1)} %broadcast_in_dim.8.taps_ref, ...), custom_call_target="tpu_custom_call" | custom-call | flops 10000000000 | bytes 786432 | tf_op jit(solution)/shard_map/student/pallas_call | solution.py:200
  44.4 0.1 constant_dynamic-update-slice_fusion.2
  44.5 0.1 constant_dynamic-update-slice_fusion.6
  44.6 0.0 collective-permute-done.1.relay_ref
  44.6 2.3 %teacher.6 = (bf16[256,384]{1,0:T(8,128)(2,1)S(1)}, bf16[256,384]{1,0:T(8,128)(2,1)S(1)}) custom-call(s32[1]{0:T(128)} %bitcast.lead_ref, bf16[256,384]{1,0:T(8,128)(2,1)S(1)} %bitcast.61, bf16[256,384]{1,0:T(8,128)(2,1)S(1)} %collective-permute-done.1.relay_ref, bf16[2,3456,384]{2,1,0:T(8,128)(2,1)S(1)} %bitcast.56), custom_call_target="tpu_custom_call" | custom-call | flops 1358954496 | bytes 5308416 | tf_op jit(solution)/shard_map/teacher/pallas_call | solution.py:53
  46.9 3.6 %collective-permute-start.2 = (bf16[256,384]{1,0:T(8,128)(2,1)S(1)}, bf16[256,384]{1,0:T(8,128)(2,1)S(1)}, u32[]{:S(2)}, u32[]{:S(2)}) collective-permute-start(bf16[256,384]{1,0:T(8,128)(2,1)S(1)} %get-tuple-element.25.teach_ref), channel_id=1, source_target_pairs={{0,2},{2,4},{4,6},{6,8},{8,10},{10,12},{12,14},{14,16},{16,18},{18... | collective-permute-start | bytes 589832 | tf_op jit(solution)/shard_map/ppermute | solution.py:246
  50.6 11.0 %student.6 = (bf16[2,256,384]{2,1,0:T(8,128)(2,1)S(1)}, bf16[2,256,384]{2,1,0:T(8,128)(2,1)S(1)}, f32[2,3,7,8,128]{4,3,2,1,0:T(8,128)S(1)}) custom-call(bf16[256,384]{1,0:T(8,128)(2,1)S(1)} %get-tuple-element.31.cur_ref, bf16[256,384]{1,0:T(8,128)(2,1)S(1)} %get-tuple-element.25.teach_ref, bf16[2,3,49,16,128]{4,3,2,1,0:T(8,128)(2,1)S(1)} %broadcast_in_dim.8.taps_ref, ...), custom_call_target="tpu_custom_call" | custom-call | flops 10000000000 | bytes 786432 | tf_op jit(solution)/shard_map/student/pallas_call | solution.py:200
  61.6 0.1 constant_dynamic-update-slice_fusion.1
  61.7 0.1 constant_dynamic-update-slice_fusion.5
  61.7 0.0 collective-permute-done.2.relay_ref
  61.8 2.3 %teacher.7 = (bf16[256,384]{1,0:T(8,128)(2,1)S(1)}, bf16[256,384]{1,0:T(8,128)(2,1)S(1)}) custom-call(s32[1]{0:T(128)} %bitcast.lead_ref, bf16[256,384]{1,0:T(8,128)(2,1)S(1)} %bitcast.60, bf16[256,384]{1,0:T(8,128)(2,1)S(1)} %collective-permute-done.2.relay_ref, bf16[2,3456,384]{2,1,0:T(8,128)(2,1)S(1)} %bitcast.57), custom_call_target="tpu_custom_call" | custom-call | flops 1358954496 | bytes 5308416 | tf_op jit(solution)/shard_map/teacher/pallas_call | solution.py:53
  64.1 11.3 %student.7 = (bf16[2,256,384]{2,1,0:T(8,128)(2,1)S(1)}, bf16[2,256,384]{2,1,0:T(8,128)(2,1)S(1)}, f32[2,3,7,8,128]{4,3,2,1,0:T(8,128)S(1)}) custom-call(bf16[256,384]{1,0:T(8,128)(2,1)S(1)} %get-tuple-element.33.cur_ref, bf16[256,384]{1,0:T(8,128)(2,1)S(1)} %get-tuple-element.26.teach_ref, bf16[2,3,49,16,128]{4,3,2,1,0:T(8,128)(2,1)S(1)} %broadcast_in_dim.8.taps_ref, ...), custom_call_target="tpu_custom_call" | custom-call | flops 10000000000 | bytes 786432 | tf_op jit(solution)/shard_map/student/pallas_call | solution.py:200
  75.4 0.2 constant_dynamic-update-slice_fusion
  75.5 0.6 fusion
  76.2 0.6 fusion.1
  76.8 0.1 copy.18
  77.0 0.1 pad_maximum_fusion
  77.0 0.2 dynamic-slice_convert_fusion
  77.2 0.1 collective-permute-start.3
  77.3 0.7 copy.16
  78.0 1.1 %collective-permute-done.3 = bf16[192,866]{0,1:T(8,128)(2,1)S(1)} collective-permute-done((bf16[192,866]{0,1:T(8,128)(2,1)S(1)}, bf16[192,866]{0,1:T(8,128)(2,1)S(1)}, u32[]{:S(2)}, u32[]{:S(2)}) %collective-permute-start.3) | collective-permute-done | bytes 332576 | tf_op jit(solution)/shard_map/ppermute | solution.py:266
  79.1 0.3 convert_add_fusion
  79.4 0.1 slice_bitcast_fusion.9
  79.5 0.1 pad_maximum_fusion.1
  79.6 1.1 %copy.19 = f32[2,384,192]{1,2,0:T(8,128)} copy(f32[2,384,192]{2,1,0:T(8,128)S(1)} %pad_maximum_fusion.1) | data formatting | bytes 1179648
  80.7 0.7 copy.20
  (17 shorter events, 0.2 us)
Async XLA Ops:
  1.6 2.5 %copy-start = (bf16[2,3,3,384,384]{4,3,2,1,0:T(8,128)(2,1)S(1)}, bf16[2,3,3,384,384]{4,3,2,1,0:T(8,128)(2,1)}, u32[]{:S(2)}) copy-start(bf16[2,3,3,384,384]{4,3,2,1,0:T(8,128)(2,1)} %param.7) | copy-start | bytes 15925252
  4.1 7.4 %copy-start.3 = (bf16[3,1,8,32,384]{4,3,2,1,0:T(8,128)(2,1)S(1)}, bf16[3,1,8,32,384]{4,3,2,1,0:T(8,128)(2,1)}, u32[]{:S(2)}) copy-start(bf16[3,1,8,32,384]{4,3,2,1,0:T(8,128)(2,1)} %param.6) | copy-start | bytes 1769476
  4.1 7.6 %copy-start.4 = (f32[2,49,384]{2,0,1:T(2,128)S(1)}, f32[2,49,384]{2,0,1:T(2,128)}, u32[]{:S(2)}) copy-start(f32[2,49,384]{2,0,1:T(2,128)} %param.8) | copy-start | bytes 451588
  6.5 5.7 %copy-start.2 = (bf16[2,384,384]{2,1,0:T(8,128)(2,1)S(1)}, bf16[2,384,384]{2,1,0:T(8,128)(2,1)}, u32[]{:S(2)}) copy-start(bf16[2,384,384]{2,1,0:T(8,128)(2,1)} %point_ref.7) | copy-start | bytes 1769476
  6.5 18.3 %collective-permute-start = (bf16[256,384]{1,0:T(8,128)(2,1)S(1)}, bf16[256,384]{1,0:T(8,128)(2,1)S(1)}, u32[]{:S(2)}, u32[]{:S(2)}) collective-permute-start(bf16[256,384]{1,0:T(8,128)(2,1)S(1)} %get-tuple-element.23.teach_ref), channel_id=1, source_target_pairs={{0,2},{2,4},{4,6},{6,8},{8,10},{10,12},{12,14},{14,16},{16,18},{18... | collective-permute-start | bytes 589832 | tf_op jit(solution)/shard_map/ppermute | solution.py:246
  24.9 2.5 %copy-start.1 = (bf16[2,3,3,384,384]{4,3,2,1,0:T(8,128)(2,1)S(1)}, bf16[2,3,3,384,384]{4,3,2,1,0:T(8,128)(2,1)}, u32[]{:S(2)}) copy-start(bf16[2,3,3,384,384]{4,3,2,1,0:T(8,128)(2,1)} %param.7) | copy-start | bytes 15925252
  27.4 17.2 %slice-start = ((s8[5308416]{0:T(1024)(128)(4,1)}), s8[4194304]{0:T(1024)(128)(4,1)S(1)}, s32[]{:S(2)}) async-start(s8[5308416]{0:T(1024)(128)(4,1)} %bitcast.54), calls=%async_computation | async-start | bytes 8388608
  29.8 14.8 %collective-permute-start.1 = (bf16[256,384]{1,0:T(8,128)(2,1)S(1)}, bf16[256,384]{1,0:T(8,128)(2,1)S(1)}, u32[]{:S(2)}, u32[]{:S(2)}) collective-permute-start(bf16[256,384]{1,0:T(8,128)(2,1)S(1)} %get-tuple-element.24.teach_ref), channel_id=1, source_target_pairs={{0,2},{2,4},{4,6},{6,8},{8,10},{10,12},{12,14},{14,16},{16,18},{18... | collective-permute-start | bytes 589832 | tf_op jit(solution)/shard_map/ppermute | solution.py:246
  33.4 11.1 %copy-start.6 = (bf16[2,1024,384]{2,1,0:T(8,128)(2,1)S(1)}, bf16[2,1024,384]{2,1,0:T(8,128)(2,1)}, u32[]{:S(2)}) copy-start(bf16[2,1024,384]{2,1,0:T(8,128)(2,1)} %constant_dynamic-update-slice_fusion.3) | copy-start | bytes 4718596
  33.4 11.1 %copy-start.5 = (bf16[2,1024,384]{2,1,0:T(8,128)(2,1)S(1)}, bf16[2,1024,384]{2,1,0:T(8,128)(2,1)}, u32[]{:S(2)}) copy-start(bf16[2,1024,384]{2,1,0:T(8,128)(2,1)} %constant_dynamic-update-slice_fusion.7) | copy-start | bytes 4718596
  33.4 11.2 %slice-start.1 = ((s8[5308416]{0:T(1024)(128)(4,1)}), s8[1114112]{0:T(1024)(128)(4,1)S(1)}, s32[]{:S(2)}) async-start(s8[5308416]{0:T(1024)(128)(4,1)} %bitcast.54), calls=%async_computation.1 | async-start | bytes 2228224
  46.9 14.8 %collective-permute-start.2 = (bf16[256,384]{1,0:T(8,128)(2,1)S(1)}, bf16[256,384]{1,0:T(8,128)(2,1)S(1)}, u32[]{:S(2)}, u32[]{:S(2)}) collective-permute-start(bf16[256,384]{1,0:T(8,128)(2,1)S(1)} %get-tuple-element.25.teach_ref), channel_id=1, source_target_pairs={{0,2},{2,4},{4,6},{6,8},{8,10},{10,12},{12,14},{14,16},{16,18},{18... | collective-permute-start | bytes 589832 | tf_op jit(solution)/shard_map/ppermute | solution.py:246
  77.2 1.9 %collective-permute-start.3 = (bf16[192,866]{0,1:T(8,128)(2,1)S(1)}, bf16[192,866]{0,1:T(8,128)(2,1)S(1)}, u32[]{:S(2)}, u32[]{:S(2)}) collective-permute-start(bf16[192,866]{0,1:T(8,128)(2,1)S(1)} %dynamic-slice_convert_fusion), channel_id=1, source_target_pairs={{0,1},{1,0},{2,3},{3,2},{4,5},{5,4},{6,7},{7,6},{8,9},{9,8},{10,11... | collective-permute-start | bytes 997640 | tf_op jit(solution)/shard_map/ppermute | solution.py:266

commit v2 on v1

--- a/solution.py
+++ b/solution.py
@@ -78,18 +78,23 @@
             two = jnp.where(keep, pltpu.roll(high, (-dy) % height, 1), 0.0)
         left = jnp.concatenate([zero, one, two[:3]], axis=0)
         right = jnp.concatenate([one[-3:], two, zero], axis=0)
-        out_ref[block, row] = jnp.concatenate([left, right], axis=1).astype(BF16)
+        out_ref[block, row] = jnp.concatenate([left, right], axis=1)
+
+
+def columns(block):
+    return pl.ds(pl.multiple_of(block * LANES, LANES), LANES)
 
 
 def tap_sum(src_ref, block, taps_ref, which, start, count, flip):
     total, held = None, None
     for row in range(7):
-        strip = src_ref[block, row, pl.ds(start, count + 6)]
+        strip = src_ref[block, row, pl.ds(start, count + 6)].astype(BF16)
         terms = []
         for col in range(7):
             tap = row * 7 + col
             tap = 48 - tap if flip else tap
-            terms.append(strip[col : col + count] * taps_ref[which, block, tap][None])
+            coef = jnp.broadcast_to(taps_ref[which, tap : tap + 1, columns(block)], strip.shape[1:])
+            terms.append(strip[col : col + count] * coef.astype(BF16)[None])
         while len(terms) > 1:
             terms = [sum(terms[i + 1 : i + 2], terms[i]) for i in range(0, len(terms), 2)]
         if held is None and row < 6:
@@ -130,15 +135,15 @@
         spread(cur_ref[:, lanes(block)].astype(F32), src0, block, height)
 
     def forward(which):
-        def chunk(index, carry):
-            for block in range(blocks):
-                act = tap_sum(srcs[which], block, taps_ref, which, index * step, step, False)
-                gel, slope = gelu_pair(act.reshape(step * pair, LANES))
-                slopes[which][span(index), lanes(block)] = slope
-                gel_ref[which, span(index), lanes(block)] = gel.astype(BF16)
+        def chunk(at, carry):
+            block, index = at // chunks, lax.rem(at, chunks)
+            act = tap_sum(srcs[which], block, taps_ref, which, index * step, step, False)
+            gel, slope = gelu_pair(act.reshape(step * pair, LANES))
+            slopes[which][span(index), columns(block)] = slope
+            gel_ref[which, span(index), columns(block)] = gel.astype(BF16)
             return carry
 
-        lax.fori_loop(0, chunks, chunk, 0)
+        lax.fori_loop(0, blocks * chunks, chunk, 0)
         return jnp.dot(gel_ref[which], point_ref[which], preferred_element_type=F32)
 
     u_one_ref[...] = forward(0) + cur_ref[...].astype(F32)
@@ -150,43 +155,43 @@
     grad_ref[1] = resid.astype(BF16)
 
     def taps_grad(which):
-        def over_rows(row, carry):
-            for block in range(blocks):
-                strip = srcs[which][block, row]
-                part = dact[:, lanes(block)].reshape(-1, pair, LANES)
-                count = part.shape[0]
-                for col in range(7):
-                    prod = strip[col : col + count] * part
-                    size = count
-                    while size > 1:
-                        size //= 2
-                        prod = prod[:size] + prod[size:]
-                    line = jnp.sum(prod[0].astype(F32), axis=0, keepdims=True)
-                    dk_ref[which, block, row, col : col + 1, :] = line
-                dk_ref[which, block, row, 7:8, :] = jnp.zeros((1, LANES), F32)
+        def over_rows(at, carry):
+            block, row = at // 7, lax.rem(at, 7)
+            strip = srcs[which][block, row].astype(BF16)
+            part = dact[:, columns(block)].reshape(-1, pair, LANES).astype(BF16)
+            count = part.shape[0]
+            for col in range(7):
+                prod = strip[col : col + count] * part
+                size = count
+                while size > 1:
+                    size //= 2
+                    prod = prod[:size] + prod[size:]
+                line = jnp.sum(prod[0].astype(F32), axis=0, keepdims=True)
+                dk_ref[which, block, row, col : col + 1, :] = line
+            dk_ref[which, block, row, 7:8, :] = jnp.zeros((1, LANES), F32)
             return carry
 
-        lax.fori_loop(0, 7, over_rows, 0)
+        lax.fori_loop(0, 7 * blocks, over_rows, 0)
 
     def back_point(which):
         dgel = lax.dot_general(grad_ref[which], point_ref[which], NT, preferred_element_type=F32)
         return dgel * slopes[which][...]
 
     dact_one = back_point(1)
-    dact[...] = dact_one.astype(BF16)
+    dact[...] = dact_one
     for block in range(blocks):
         spread(dact_one[:, lanes(block)], src2, block, height)
 
-    def chunk_back(index, carry):
-        for block in range(blocks):
-            back = tap_sum(src2, block, taps_ref, 1, index * step, step, True)
-            back = back.reshape(step * pair, LANES) + resid_ref[span(index), lanes(block)]
-            grad_ref[0, span(index), lanes(block)] = back.astype(BF16)
+    def chunk_back(at, carry):
+        block, index = at // chunks, lax.rem(at, chunks)
+        back = tap_sum(src2, block, taps_ref, 1, index * step, step, True)
+        back = back.reshape(step * pair, LANES) + resid_ref[span(index), columns(block)]
+        grad_ref[0, span(index), columns(block)] = back.astype(BF16)
         return carry
 
-    lax.fori_loop(0, chunks, chunk_back, 0)
+    lax.fori_loop(0, blocks * chunks, chunk_back, 0)
     taps_grad(1)
-    dact[...] = back_point(0).astype(BF16)
+    dact[...] = back_point(0)
     taps_grad(0)
 
 
@@ -195,7 +200,7 @@
     blocks = chans // LANES
     half = rows // (2 * height)
     vmem = pl.BlockSpec(memory_space=pltpu.VMEM)
-    spread_shape = pltpu.VMEM((blocks, 7, half + 6, 2 * height, LANES), BF16)
+    spread_shape = pltpu.VMEM((blocks, 7, half + 6, 2 * height, LANES), F32)
     map_shape = pltpu.VMEM((rows, chans), F32)
     return pl.pallas_call(
         functools.partial(student_kernel, height, half // 2),
@@ -208,8 +213,7 @@
         out_specs=(vmem,) * 3,
         scratch_shapes=[spread_shape] * 3
         + [map_shape] * 2
-        + [pltpu.VMEM((rows, chans), BF16)]
-        + [map_shape] * 2,
+        + [map_shape] * 3,
         compiler_params=pltpu.CompilerParams(vmem_limit_bytes=32 << 20),
         cost_estimate=pl.CostEstimate(
             flops=10_000_000_000, bytes_accessed=8 * rows * chans, transcendentals=0
@@ -234,8 +238,6 @@
     relay = to_rows(pipe_maps[0, 0])
     fresh = to_rows(fresh_maps[:, 0])
     weight = teacher_weight.reshape(2, 9 * chans, chans)
-    taps = student_depth.astype(BF16).reshape(2, -1, blocks, 1, LANES).swapaxes(1, 2)
-    taps = jnp.broadcast_to(taps, taps.shape[:3] + (2 * height, LANES))
     ticks = fresh_maps.shape[0] + 1
     gels, grads, depth_total = [], [], None
     teach = relay
@@ -244,7 +246,7 @@
         teach, current = teacher(lead, mine, relay, weight, height)
         if tick + 1 < ticks:
             relay = lax.ppermute(teach, "section", route)
-        gel, grad, part = student(current, teach, taps, student_point, height)
+        gel, grad, part = student(current, teach, student_depth, student_point, height)
         gels.append(gel)
         grads.append(grad)
         depth_total = part if depth_total is None else depth_total + part

time: 81.6 us -> 68.9 us (0.84)
  Pallas kernels: 53.8 us -> 41.7 us
    pallas_call x4, Pallas kernels: 44.4 us -> 32.3 us  [student(): pl.pallas_call(functools.partial(student_kernel, height, half // 2), out_...]
    unnamed x28 -> x29, local copies, waits for them, and re-layouts: 8.7 us -> 8.71 us
  transfers between devices with their start and end apart: 4 -> 4, of which waited for: 1 -> 1; matrix products, arithmetic and copies ran while one was open for 4% -> 4% of each run, Pallas kernels for 41% -> 35%
where the time goes in v2:
time: 68.9 us; the launch traced here: 68.6 us
  Pallas kernels  41.7 us (61%)
  starting transfers between devices  11.9 us (17%)
  local copies, waits for them, and re-layouts  11.1 us (16%)
  matrix products  1.24 us (2%)
  waiting for transfers between devices  1.07 us (2%)
  between operations  0.98 us (1%)
    pallas_call x4, Pallas kernels, student(): pl.pallas_call(functools.partial(student_kernel, height, half // 2), out_...  32.3 us
    ppermute x3, starting transfers between devices, body(): relay = lax.ppermute(teach, 'section', route)  11.9 us
    pallas_call x4, Pallas kernels, teacher(): pl.pallas_call(functools.partial(teacher_kernel, height), out_shape=(jax....  9.38 us
    unnamed x29, local copies, waits for them, and re-layouts  8.71 us
  transfers between devices with their start and end apart: 4, of which 1 were waited for; matrix products, arithmetic and copies ran while one was open for 4% of the time, Pallas kernels for 35%

profile of v2, /device:TPU:0, one launch (start us, length us, event | category | flops | bytes accessed | tf_op | source)
XLA Modules:
  0.0 68.6 jit_solution(5514881762100513124)
XLA Ops:
  0.6 1.0 %copy.18 = bf16[8,2,16,384]{3,0,1,2:T(8,128)(2,1)S(1)} copy(bf16[8,2,16,384]{3,2,1,0:T(8,128)(2,1)} %bitcast.64) | data formatting | bytes 393216 | tf_op jit(solution)/shard_map/reshape;squeeze | solution.py:235
  1.6 0.0 copy-start
  1.6 2.5 %copy-done = bf16[2,3,3,384,384]{4,3,2,1,0:T(8,128)(2,1)S(1)} copy-done((bf16[2,3,3,384,384]{4,3,2,1,0:T(8,128)(2,1)S(1)}, bf16[2,3,3,384,384]{4,3,2,1,0:T(8,128)(2,1)}, u32[]{:S(2)}) %copy-start) | copy-done | bytes 5308440
  4.1 2.4 %teacher.4 = (bf16[256,384]{1,0:T(8,128)(2,1)S(1)}, bf16[256,384]{1,0:T(8,128)(2,1)S(1)}) custom-call(s32[1]{0:T(128)} %bitcast.lead_ref, bf16[256,384]{1,0:T(8,128)(2,1)S(1)} %bitcast.53, bf16[256,384]{1,0:T(8,128)(2,1)S(1)} %bitcast.54, bf16[2,3456,384]{2,1,0:T(8,128)(2,1)S(1)} %bitcast.47), custom_call_target="tpu_custom_call" | custom-call | flops 1358954496 | bytes 5308416 | tf_op jit(solution)/shard_map/teacher/pallas_call | solution.py:53
  6.5 4.9 %collective-permute-start = (bf16[256,384]{1,0:T(8,128)(2,1)S(1)}, bf16[256,384]{1,0:T(8,128)(2,1)S(1)}, u32[]{:S(2)}, u32[]{:S(2)}) collective-permute-start(bf16[256,384]{1,0:T(8,128)(2,1)S(1)} %get-tuple-element.23.teach_ref), channel_id=1, source_target_pairs={{0,2},{2,4},{4,6},{6,8},{8,10},{10,12},{12,14},{14,16},{16,18},{18... | collective-permute-start | bytes 589832 | tf_op jit(solution)/shard_map/ppermute | solution.py:248
  11.4 0.0 copy-done.3
  11.4 0.2 copy.29
  11.6 0.0 copy-done.4
  11.7 0.0 copy-done.2
  11.7 8.1 %student.4 = (bf16[2,256,384]{2,1,0:T(8,128)(2,1)S(1)}, bf16[2,256,384]{2,1,0:T(8,128)(2,1)S(1)}, f32[2,3,7,8,128]{4,3,2,1,0:T(8,128)S(1)}) custom-call(bf16[256,384]{1,0:T(8,128)(2,1)S(1)} %get-tuple-element.27.cur_ref, bf16[256,384]{1,0:T(8,128)(2,1)S(1)} %get-tuple-element.23.teach_ref, f32[2,49,384]{2,1,0:T(8,128)S(1)} %copy.20.taps_ref, ...), custom_call_target="tpu_custom_call" | custom-call | flops 10000000000 | bytes 786432 | tf_op jit(solution)/shard_map/student/pallas_call | solution.py:205
  19.8 0.8 %constant_dynamic-update-slice_fusion.3 = bf16[2,1024,384]{2,1,0:T(8,128)(2,1)} fusion(bf16[2,256,384]{2,1,0:T(8,128)(2,1)S(1)} %get-tuple-element.28), kind=kLoop, calls=%fused_computation.21 | loop fusion | bytes 786432
  20.6 0.8 %constant_dynamic-update-slice_fusion.7 = bf16[2,1024,384]{2,1,0:T(8,128)(2,1)} fusion(bf16[2,256,384]{2,1,0:T(8,128)(2,1)S(1)} %get-tuple-element.35), kind=kLoop, calls=%fused_computation.25 | loop fusion | bytes 786432
  21.4 0.1 fusion.3
  21.4 0.0 collective-permute-done.relay_ref
  21.4 0.0 copy-start.1
  21.4 2.5 %copy-done.1 = bf16[2,3,3,384,384]{4,3,2,1,0:T(8,128)(2,1)S(1)} copy-done((bf16[2,3,3,384,384]{4,3,2,1,0:T(8,128)(2,1)S(1)}, bf16[2,3,3,384,384]{4,3,2,1,0:T(8,128)(2,1)}, u32[]{:S(2)}) %copy-start.1) | copy-done | bytes 5308440
  23.9 2.4 %teacher.5 = (bf16[256,384]{1,0:T(8,128)(2,1)S(1)}, bf16[256,384]{1,0:T(8,128)(2,1)S(1)}) custom-call(s32[1]{0:T(128)} %bitcast.lead_ref, bf16[256,384]{1,0:T(8,128)(2,1)S(1)} %bitcast.57, bf16[256,384]{1,0:T(8,128)(2,1)S(1)} %collective-permute-done.relay_ref, bf16[2,3456,384]{2,1,0:T(8,128)(2,1)S(1)} %bitcast.48), custom_call_target="tpu_custom_call" | custom-call | flops 1358954496 | bytes 5308416 | tf_op jit(solution)/shard_map/teacher/pallas_call | solution.py:53
  26.3 3.4 %collective-permute-start.1 = (bf16[256,384]{1,0:T(8,128)(2,1)S(1)}, bf16[256,384]{1,0:T(8,128)(2,1)S(1)}, u32[]{:S(2)}, u32[]{:S(2)}) collective-permute-start(bf16[256,384]{1,0:T(8,128)(2,1)S(1)} %get-tuple-element.24.teach_ref), channel_id=1, source_target_pairs={{0,2},{2,4},{4,6},{6,8},{8,10},{10,12},{12,14},{14,16},{16,18},{18... | collective-permute-start | bytes 589832 | tf_op jit(solution)/shard_map/ppermute | solution.py:248
  29.7 0.0 copy-start.6
  29.7 0.0 copy-start.5
  29.7 0.0 slice-start.1
  29.8 8.1 %student.5 = (bf16[2,256,384]{2,1,0:T(8,128)(2,1)S(1)}, bf16[2,256,384]{2,1,0:T(8,128)(2,1)S(1)}, f32[2,3,7,8,128]{4,3,2,1,0:T(8,128)S(1)}) custom-call(bf16[256,384]{1,0:T(8,128)(2,1)S(1)} %get-tuple-element.29.cur_ref, bf16[256,384]{1,0:T(8,128)(2,1)S(1)} %get-tuple-element.24.teach_ref, f32[2,49,384]{2,1,0:T(8,128)S(1)} %copy.20.taps_ref, ...), custom_call_target="tpu_custom_call" | custom-call | flops 10000000000 | bytes 786432 | tf_op jit(solution)/shard_map/student/pallas_call | solution.py:205
  37.9 0.1 constant_dynamic-update-slice_fusion.2
  37.9 0.0 copy-done.5
  37.9 0.1 constant_dynamic-update-slice_fusion.6
  38.0 0.0 collective-permute-done.1.relay_ref
  38.1 2.3 %teacher.6 = (bf16[256,384]{1,0:T(8,128)(2,1)S(1)}, bf16[256,384]{1,0:T(8,128)(2,1)S(1)}) custom-call(s32[1]{0:T(128)} %bitcast.lead_ref, bf16[256,384]{1,0:T(8,128)(2,1)S(1)} %bitcast.56, bf16[256,384]{1,0:T(8,128)(2,1)S(1)} %collective-permute-done.1.relay_ref, bf16[2,3456,384]{2,1,0:T(8,128)(2,1)S(1)} %bitcast.51), custom_call_target="tpu_custom_call" | custom-call | flops 1358954496 | bytes 5308416 | tf_op jit(solution)/shard_map/teacher/pallas_call | solution.py:53
  40.4 3.6 %collective-permute-start.2 = (bf16[256,384]{1,0:T(8,128)(2,1)S(1)}, bf16[256,384]{1,0:T(8,128)(2,1)S(1)}, u32[]{:S(2)}, u32[]{:S(2)}) collective-permute-start(bf16[256,384]{1,0:T(8,128)(2,1)S(1)} %get-tuple-element.25.teach_ref), channel_id=1, source_target_pairs={{0,2},{2,4},{4,6},{6,8},{8,10},{10,12},{12,14},{14,16},{16,18},{18... | collective-permute-start | bytes 589832 | tf_op jit(solution)/shard_map/ppermute | solution.py:248
  44.0 8.1 %student.6 = (bf16[2,256,384]{2,1,0:T(8,128)(2,1)S(1)}, bf16[2,256,384]{2,1,0:T(8,128)(2,1)S(1)}, f32[2,3,7,8,128]{4,3,2,1,0:T(8,128)S(1)}) custom-call(bf16[256,384]{1,0:T(8,128)(2,1)S(1)} %get-tuple-element.31.cur_ref, bf16[256,384]{1,0:T(8,128)(2,1)S(1)} %get-tuple-element.25.teach_ref, f32[2,49,384]{2,1,0:T(8,128)S(1)} %copy.20.taps_ref, ...), custom_call_target="tpu_custom_call" | custom-call | flops 10000000000 | bytes 786432 | tf_op jit(solution)/shard_map/student/pallas_call | solution.py:205
  52.0 0.1 constant_dynamic-update-slice_fusion.1
  52.1 0.1 constant_dynamic-update-slice_fusion.5
  52.2 0.0 collective-permute-done.2.relay_ref
  52.2 2.3 %teacher.7 = (bf16[256,384]{1,0:T(8,128)(2,1)S(1)}, bf16[256,384]{1,0:T(8,128)(2,1)S(1)}) custom-call(s32[1]{0:T(128)} %bitcast.lead_ref, bf16[256,384]{1,0:T(8,128)(2,1)S(1)} %bitcast.55, bf16[256,384]{1,0:T(8,128)(2,1)S(1)} %collective-permute-done.2.relay_ref, bf16[2,3456,384]{2,1,0:T(8,128)(2,1)S(1)} %bitcast.52), custom_call_target="tpu_custom_call" | custom-call | flops 1358954496 | bytes 5308416 | tf_op jit(solution)/shard_map/teacher/pallas_call | solution.py:53
  54.5 8.1 %student.7 = (bf16[2,256,384]{2,1,0:T(8,128)(2,1)S(1)}, bf16[2,256,384]{2,1,0:T(8,128)(2,1)S(1)}, f32[2,3,7,8,128]{4,3,2,1,0:T(8,128)S(1)}) custom-call(bf16[256,384]{1,0:T(8,128)(2,1)S(1)} %get-tuple-element.33.cur_ref, bf16[256,384]{1,0:T(8,128)(2,1)S(1)} %get-tuple-element.26.teach_ref, f32[2,49,384]{2,1,0:T(8,128)S(1)} %copy.20.taps_ref, ...), custom_call_target="tpu_custom_call" | custom-call | flops 10000000000 | bytes 786432 | tf_op jit(solution)/shard_map/student/pallas_call | solution.py:205
  62.6 0.2 constant_dynamic-update-slice_fusion
  62.8 0.6 fusion
  63.4 0.6 fusion.1
  64.1 0.1 copy.24
  64.2 0.1 pad_maximum_fusion
  64.3 0.2 dynamic-slice_convert_fusion
  64.5 0.1 collective-permute-start.3
  64.6 0.7 %copy.19 = bf16[8,2,16,384]{3,2,1,0:T(8,128)(2,1)} copy(bf16[8,2,16,384]{3,0,1,2:T(8,128)(2,1)S(1)} %bitcast.58) | data formatting | bytes 393216 | tf_op jit(solution)/shard_map/transpose | solution.py:271
  65.3 1.1 %collective-permute-done.3 = bf16[192,866]{0,1:T(8,128)(2,1)S(1)} collective-permute-done((bf16[192,866]{0,1:T(8,128)(2,1)S(1)}, bf16[192,866]{0,1:T(8,128)(2,1)S(1)}, u32[]{:S(2)}, u32[]{:S(2)}) %collective-permute-start.3) | collective-permute-done | bytes 332576 | tf_op jit(solution)/shard_map/ppermute | solution.py:268
  66.3 0.3 convert_add_fusion
  66.7 0.1 slice_bitcast_fusion.9
  66.8 0.1 pad_maximum_fusion.1
  66.8 1.1 %copy.25 = f32[2,384,192]{1,2,0:T(8,128)} copy(f32[2,384,192]{2,1,0:T(8,128)S(1)} %pad_maximum_fusion.1) | data formatting | bytes 1179648
  67.9 0.7 %copy.26 = f32[2,49,192]{2,0,1:T(2,128)} copy(f32[2,49,192]{2,1,0:T(8,128)S(1)} %reshape.43) | data formatting | bytes 150528
  (14 shorter events, 0.1 us)
Async XLA Ops:
  1.6 2.5 %copy-start = (bf16[2,3,3,384,384]{4,3,2,1,0:T(8,128)(2,1)S(1)}, bf16[2,3,3,384,384]{4,3,2,1,0:T(8,128)(2,1)}, u32[]{:S(2)}) copy-start(bf16[2,3,3,384,384]{4,3,2,1,0:T(8,128)(2,1)} %param.7) | copy-start | bytes 15925252
  4.1 7.3 %copy-start.3 = (bf16[3,1,8,32,384]{4,3,2,1,0:T(8,128)(2,1)S(1)}, bf16[3,1,8,32,384]{4,3,2,1,0:T(8,128)(2,1)}, u32[]{:S(2)}) copy-start(bf16[3,1,8,32,384]{4,3,2,1,0:T(8,128)(2,1)} %param.6) | copy-start | bytes 1769476
  4.1 7.5 %copy-start.4 = (f32[2,49,384]{2,0,1:T(2,128)S(1)}, f32[2,49,384]{2,0,1:T(2,128)}, u32[]{:S(2)}) copy-start(f32[2,49,384]{2,0,1:T(2,128)} %param.8) | copy-start | bytes 451588
  4.1 7.5 %copy-start.2 = (bf16[2,384,384]{2,1,0:T(8,128)(2,1)S(1)}, bf16[2,384,384]{2,1,0:T(8,128)(2,1)}, u32[]{:S(2)}) copy-start(bf16[2,384,384]{2,1,0:T(8,128)(2,1)} %point_ref.7) | copy-start | bytes 1769476
  6.5 14.9 %collective-permute-start = (bf16[256,384]{1,0:T(8,128)(2,1)S(1)}, bf16[256,384]{1,0:T(8,128)(2,1)S(1)}, u32[]{:S(2)}, u32[]{:S(2)}) collective-permute-start(bf16[256,384]{1,0:T(8,128)(2,1)S(1)} %get-tuple-element.23.teach_ref), channel_id=1, source_target_pairs={{0,2},{2,4},{4,6},{6,8},{8,10},{10,12},{12,14},{14,16},{16,18},{18... | collective-permute-start | bytes 589832 | tf_op jit(solution)/shard_map/ppermute | solution.py:248
  21.4 2.5 %copy-start.1 = (bf16[2,3,3,384,384]{4,3,2,1,0:T(8,128)(2,1)S(1)}, bf16[2,3,3,384,384]{4,3,2,1,0:T(8,128)(2,1)}, u32[]{:S(2)}) copy-start(bf16[2,3,3,384,384]{4,3,2,1,0:T(8,128)(2,1)} %param.7) | copy-start | bytes 15925252
  23.9 14.1 %slice-start = ((s8[5308416]{0:T(1024)(128)(4,1)}), s8[4194304]{0:T(1024)(128)(4,1)S(1)}, s32[]{:S(2)}) async-start(s8[5308416]{0:T(1024)(128)(4,1)} %bitcast.49), calls=%async_computation | async-start | bytes 8388608
  26.3 11.7 %collective-permute-start.1 = (bf16[256,384]{1,0:T(8,128)(2,1)S(1)}, bf16[256,384]{1,0:T(8,128)(2,1)S(1)}, u32[]{:S(2)}, u32[]{:S(2)}) collective-permute-start(bf16[256,384]{1,0:T(8,128)(2,1)S(1)} %get-tuple-element.24.teach_ref), channel_id=1, source_target_pairs={{0,2},{2,4},{4,6},{6,8},{8,10},{10,12},{12,14},{14,16},{16,18},{18... | collective-permute-start | bytes 589832 | tf_op jit(solution)/shard_map/ppermute | solution.py:248
  29.7 8.1 %copy-start.6 = (bf16[2,1024,384]{2,1,0:T(8,128)(2,1)S(1)}, bf16[2,1024,384]{2,1,0:T(8,128)(2,1)}, u32[]{:S(2)}) copy-start(bf16[2,1024,384]{2,1,0:T(8,128)(2,1)} %constant_dynamic-update-slice_fusion.3) | copy-start | bytes 4718596
  29.7 8.2 %copy-start.5 = (bf16[2,1024,384]{2,1,0:T(8,128)(2,1)S(1)}, bf16[2,1024,384]{2,1,0:T(8,128)(2,1)}, u32[]{:S(2)}) copy-start(bf16[2,1024,384]{2,1,0:T(8,128)(2,1)} %constant_dynamic-update-slice_fusion.7) | copy-start | bytes 4718596
  29.7 8.3 %slice-start.1 = ((s8[5308416]{0:T(1024)(128)(4,1)}), s8[1114112]{0:T(1024)(128)(4,1)S(1)}, s32[]{:S(2)}) async-start(s8[5308416]{0:T(1024)(128)(4,1)} %bitcast.49), calls=%async_computation.1 | async-start | bytes 2228224
  40.4 11.8 %collective-permute-start.2 = (bf16[256,384]{1,0:T(8,128)(2,1)S(1)}, bf16[256,384]{1,0:T(8,128)(2,1)S(1)}, u32[]{:S(2)}, u32[]{:S(2)}) collective-permute-start(bf16[256,384]{1,0:T(8,128)(2,1)S(1)} %get-tuple-element.25.teach_ref), channel_id=1, source_target_pairs={{0,2},{2,4},{4,6},{6,8},{8,10},{10,12},{12,14},{14,16},{16,18},{18... | collective-permute-start | bytes 589832 | tf_op jit(solution)/shard_map/ppermute | solution.py:248
  64.5 1.9 %collective-permute-start.3 = (bf16[192,866]{0,1:T(8,128)(2,1)S(1)}, bf16[192,866]{0,1:T(8,128)(2,1)S(1)}, u32[]{:S(2)}, u32[]{:S(2)}) collective-permute-start(bf16[192,866]{0,1:T(8,128)(2,1)S(1)} %dynamic-slice_convert_fusion), channel_id=1, source_target_pairs={{0,1},{1,0},{2,3},{3,2},{4,5},{5,4},{6,7},{7,6},{8,9},{9,8},{10,11... | collective-permute-start | bytes 997640 | tf_op jit(solution)/shard_map/ppermute | solution.py:268

commit v3 on v2

--- a/solution.py
+++ b/solution.py
@@ -10,6 +10,7 @@
 LANES = 128
 F32 = jnp.float32
 BF16 = jnp.bfloat16
+MESH = pl.DeviceIdType.MESH
 NT = (((1,), (1,)), ((), ()))
 
 
@@ -56,7 +57,7 @@
         in_specs=[pl.BlockSpec(memory_space=pltpu.SMEM), vmem, vmem, vmem],
         out_specs=(vmem, vmem),
         scratch_shapes=[pltpu.VMEM((rows, 9 * chans), BF16)],
-        compiler_params=pltpu.CompilerParams(vmem_limit_bytes=24 << 20),
+        compiler_params=pltpu.CompilerParams(vmem_limit_bytes=12 << 20),
         cost_estimate=pl.CostEstimate(
             flops=2 * 2 * 9 * rows * chans * chans, bytes_accessed=weight.size * 2, transcendentals=0
         ),
@@ -116,9 +117,30 @@
 
 
 def student_kernel(
-    height, step, cur_ref, teach_ref, taps_ref, point_ref,
-    gel_ref, grad_ref, dk_ref, src0, src1, src2, slope0, slope1, dact, u_one_ref, resid_ref,
+    height, step, sections, cur_ref, teach_ref, taps_ref, point_ref,
+    gel0, gel1, grad0, grad1, dk_ref, *rest,
 ):
+    if sections:
+        relay_ref, *rest = rest
+        *rest, land, send_sem, recv_sem = rest
+        spot = lax.axis_index("section")
+        later, earlier = lax.rem(spot + 1, sections), lax.rem(spot + sections - 1, sections)
+        barrier = pltpu.get_barrier_semaphore()
+
+        @pl.when(spot > 0)
+        def _():
+            pl.semaphore_signal(barrier, inc=1, device_id={"section": earlier}, device_id_type=MESH)
+
+        copy = pltpu.make_async_remote_copy(
+            src_ref=teach_ref,
+            dst_ref=land,
+            send_sem=send_sem,
+            recv_sem=recv_sem,
+            device_id={"section": later},
+            device_id_type=MESH,
+        )
+    src0, src1, src2, slope0, slope1, dact, u_one_ref, resid_ref = rest
+    gels, grads = (gel0, gel1), (grad0, grad1)
     rows, chans = cur_ref.shape
     blocks = chans // LANES
     pair = 2 * height
@@ -140,19 +162,26 @@
             act = tap_sum(srcs[which], block, taps_ref, which, index * step, step, False)
             gel, slope = gelu_pair(act.reshape(step * pair, LANES))
             slopes[which][span(index), columns(block)] = slope
-            gel_ref[which, span(index), columns(block)] = gel.astype(BF16)
+            gels[which][span(index), columns(block)] = gel.astype(BF16)
             return carry
 
         lax.fori_loop(0, blocks * chunks, chunk, 0)
-        return jnp.dot(gel_ref[which], point_ref[which], preferred_element_type=F32)
+        return jnp.dot(gels[which][...], point_ref[which], preferred_element_type=F32)
 
     u_one_ref[...] = forward(0) + cur_ref[...].astype(F32)
     for block in range(blocks):
         spread(u_one_ref[:, lanes(block)], src1, block, height)
+    if sections:
+
+        @pl.when(spot < sections - 1)
+        def _():
+            pl.semaphore_wait(barrier, 1)
+            copy.start()
+
     diff = forward(1) + u_one_ref[...] - teach_ref[...].astype(F32)
     resid = diff * (4.0 / rows)
     resid_ref[...] = resid
-    grad_ref[1] = resid.astype(BF16)
+    grad1[...] = resid.astype(BF16)
 
     def taps_grad(which):
         def over_rows(at, carry):
@@ -174,7 +203,7 @@
         lax.fori_loop(0, 7 * blocks, over_rows, 0)
 
     def back_point(which):
-        dgel = lax.dot_general(grad_ref[which], point_ref[which], NT, preferred_element_type=F32)
+        dgel = lax.dot_general(grads[which][...], point_ref[which], NT, preferred_element_type=F32)
         return dgel * slopes[which][...]
 
     dact_one = back_point(1)
@@ -186,35 +215,51 @@
         block, index = at // chunks, lax.rem(at, chunks)
         back = tap_sum(src2, block, taps_ref, 1, index * step, step, True)
         back = back.reshape(step * pair, LANES) + resid_ref[span(index), columns(block)]
-        grad_ref[0, span(index), columns(block)] = back.astype(BF16)
+        grad0[span(index), columns(block)] = back.astype(BF16)
         return carry
 
     lax.fori_loop(0, blocks * chunks, chunk_back, 0)
     taps_grad(1)
     dact[...] = back_point(0)
     taps_grad(0)
-
-
-def student(current, teach, taps, point, height):
+    if sections:
+
+        @pl.when(spot > 0)
+        def _():
+            copy.wait_recv()
+            relay_ref[...] = land[...]
+
+        @pl.when(spot == 0)
+        def _():
+            relay_ref[...] = jnp.zeros_like(relay_ref)
+
+        @pl.when(spot < sections - 1)
+        def _():
+            copy.wait_send()
+
+
+def student(current, teach, taps, point, height, sections):
     rows, chans = current.shape
     blocks = chans // LANES
     half = rows // (2 * height)
     vmem = pl.BlockSpec(memory_space=pltpu.VMEM)
     spread_shape = pltpu.VMEM((blocks, 7, half + 6, 2 * height, LANES), F32)
     map_shape = pltpu.VMEM((rows, chans), F32)
+    flat = jax.ShapeDtypeStruct((rows, chans), BF16)
+    outs = [flat] * 4 + [jax.ShapeDtypeStruct((2, blocks, 7, 8, LANES), F32)]
+    scratch = [spread_shape] * 3 + [map_shape] * 5
+    params = {}
+    if sections:
+        outs.append(flat)
+        scratch += [pltpu.VMEM((rows, chans), BF16), pltpu.SemaphoreType.DMA, pltpu.SemaphoreType.DMA]
+        params = {"collective_id": 0, "has_side_effects": True}
     return pl.pallas_call(
-        functools.partial(student_kernel, height, half // 2),
-        out_shape=(
-            jax.ShapeDtypeStruct((2, rows, chans), BF16),
-            jax.ShapeDtypeStruct((2, rows, chans), BF16),
-            jax.ShapeDtypeStruct((2, blocks, 7, 8, LANES), F32),
-        ),
+        functools.partial(student_kernel, height, half // 2, sections),
+        out_shape=tuple(outs),
         in_specs=[vmem] * 4,
-        out_specs=(vmem,) * 3,
-        scratch_shapes=[spread_shape] * 3
-        + [map_shape] * 2
-        + [map_shape] * 3,
-        compiler_params=pltpu.CompilerParams(vmem_limit_bytes=32 << 20),
+        out_specs=(vmem,) * len(outs),
+        scratch_shapes=scratch,
+        compiler_params=pltpu.CompilerParams(vmem_limit_bytes=22 << 20, **params),
         cost_estimate=pl.CostEstimate(
             flops=10_000_000_000, bytes_accessed=8 * rows * chans, transcendentals=0
         ),
@@ -228,7 +273,6 @@
     blocks = chans // LANES
     lead = (lax.axis_index("section") == 0).astype(jnp.int32).reshape(1)
     sections = lax.axis_size("section")
-    route = [(i, i + 1) for i in range(sections - 1)]
 
     def to_rows(maps):
         front = maps.shape[:-3]
@@ -244,14 +288,17 @@
     for tick in range(ticks):
         mine = relay if tick == 0 else fresh[tick - 1]
         teach, current = teacher(lead, mine, relay, weight, height)
-        if tick + 1 < ticks:
-            relay = lax.ppermute(teach, "section", route)
-        gel, grad, part = student(current, teach, student_depth, student_point, height)
-        gels.append(gel)
-        grads.append(grad)
+        linked = sections if tick + 1 < ticks else 0
+        gel0, gel1, grad0, grad1, part, *sent = student(
+            current, teach, student_depth, student_point, height, linked
+        )
+        if sent:
+            relay = sent[0]
+        gels.append((gel0, gel1))
+        grads.append((grad0, grad1))
         depth_total = part if depth_total is None else depth_total + part
-    gel_all = jnp.concatenate(gels, axis=1)
-    grad_all = jnp.concatenate(grads, axis=1)
+    gel_all = [jnp.concatenate([pair[b] for pair in gels]) for b in range(2)]
+    grad_all = [jnp.concatenate([pair[b] for pair in grads]) for b in range(2)]
     point_total = [
         lax.dot_general(grad_all[b], gel_all[b], (((0,), (0,)), ((), ())), preferred_element_type=F32)
         for b in range(2)

time: 68.9 us -> 54.2 us (0.79)
  starting transfers between devices: 11.9 us -> 0.07 us
  local copies, waits for them, and re-layouts: 11.1 us -> 6.82 us
  Pallas kernels: 41.7 us -> 43 us
    ppermute x3 -> x0, starting transfers between devices: 11.9 us -> none  [body(): relay = lax.ppermute(teach, 'section', route)]
    unnamed x29 -> x17, local copies, waits for them, and re-layouts: 8.71 us -> 4.35 us
    pallas_call x4, Pallas kernels: 32.3 us -> 33.7 us  [student(): pl.pallas_call(functools.partial(student_kernel, height, half // 2, secti...]
  transfers between devices with their start and end apart: 4 -> 1, of which waited for: 1 -> 1; matrix products, arithmetic and copies ran while one was open for 4% -> 1% of each run, Pallas kernels for 35% -> 0%
where the time goes in v3:
time: 54.2 us; the launch traced here: 53.6 us
  Pallas kernels  43 us (79%)
  local copies, waits for them, and re-layouts  6.82 us (13%)
  matrix products  1.24 us (2%)
  waiting for transfers between devices  1.07 us (2%)
  between operations  0.88 us (2%)
    pallas_call x4, Pallas kernels, student(): pl.pallas_call(functools.partial(student_kernel, height, half // 2, secti...  33.7 us
    pallas_call x4, Pallas kernels, teacher(): pl.pallas_call(functools.partial(teacher_kernel, height), out_shape=(jax....  9.32 us
    unnamed x17, local copies, waits for them, and re-layouts  4.35 us
    another operation x2, local copies, waits for them, and re-layouts, to_rows(): split = maps.reshape(front + (height, 2, width // 2, chans))  1.37 us
    dot_general x2, matrix products, body(): lax.dot_general(grad_all[b], gel_all[b], (((0,), (0,)), ((), ())), prefer...  1.24 us
  transfers between devices with their start and end apart: 1, of which 1 were waited for; matrix products, arithmetic and copies ran while one was open for 1% of the time, Pallas kernels for 0%

profile of v3, /device:TPU:0, one launch (start us, length us, event | category | flops | bytes accessed | tf_op | source)
XLA Modules:
  0.0 53.6 jit_solution(3505052311241535294)
XLA Ops:
  0.6 0.0 copy-start.2
  0.6 0.0 copy-start.3
  0.7 1.3 %copy.29 = bf16[3,8,2,16,384]{4,1,2,3,0:T(8,128)(2,1)S(1)} copy(bf16[3,8,2,16,384]{4,3,2,1,0:T(8,128)(2,1)} %bitcast.51) | data formatting | bytes 1179648 | tf_op jit(solution)/shard_map/reshape;squeeze | solution.py:279
  2.0 0.1 fusion.33
  2.0 0.0 copy-done.2
  2.0 0.1 copy.18
  2.1 0.0 copy-done.3
  2.2 0.0 copy-start
  2.2 2.5 %copy-done = bf16[2,3,3,384,384]{4,3,2,1,0:T(8,128)(2,1)S(1)} copy-done((bf16[2,3,3,384,384]{4,3,2,1,0:T(8,128)(2,1)S(1)}, bf16[2,3,3,384,384]{4,3,2,1,0:T(8,128)(2,1)}, u32[]{:S(2)}) %copy-start) | copy-done | bytes 5308440
  4.7 0.0 copy-start.1
  4.7 0.0 slice-start
  4.7 2.4 %teacher.4 = (bf16[256,384]{1,0:T(8,128)(2,1)S(1)}, bf16[256,384]{1,0:T(8,128)(2,1)S(1)}) custom-call(s32[1]{0:T(128)} %bitcast.lead_ref, bf16[256,384]{1,0:T(8,128)(2,1)S(1)} %bitcast.41, bf16[256,384]{1,0:T(8,128)(2,1)S(1)} %bitcast.42, bf16[2,3456,384]{2,1,0:T(8,128)(2,1)S(1)} %bitcast.35), custom_call_target="tpu_custom_call" | custom-call | flops 1358954496 | bytes 5308416 | tf_op jit(solution)/shard_map/teacher/pallas_call | solution.py:54
  7.0 0.0 copy-done.1
  7.1 0.0 slice-start.1
  7.1 9.1 %student.4 = (bf16[256,384]{1,0:T(8,128)(2,1)S(1)}, bf16[256,384]{1,0:T(8,128)(2,1)S(1)}, bf16[256,384]{1,0:T(8,128)(2,1)S(1)}, bf16[256,384]{1,0:T(8,128)(2,1)S...) custom-call(bf16[256,384]{1,0:T(8,128)(2,1)S(1)} %get-tuple-element.34.cur_ref, ...), custom_call_target="tpu_custom_call" | custom-call | flops 10000000000 | bytes 786432 | tf_op jit(solution)/shard_map/student/pallas_call | solution.py:256
  16.2 0.0 slice-done
  16.2 0.0 slice-done.1
  16.2 2.3 %teacher.5 = (bf16[256,384]{1,0:T(8,128)(2,1)S(1)}, bf16[256,384]{1,0:T(8,128)(2,1)S(1)}) custom-call(s32[1]{0:T(128)} %bitcast.lead_ref, bf16[256,384]{1,0:T(8,128)(2,1)S(1)} %bitcast.45, bf16[256,384]{1,0:T(8,128)(2,1)S(1)} %get-tuple-element.36.relay_ref, bf16[2,3456,384]{2,1,0:T(8,128)(2,1)S(1)} %bitcast.38), custom_call_target="tpu_custom_call" | custom-call | flops 1358954496 | bytes 5308416 | tf_op jit(solution)/shard_map/teacher/pallas_call | solution.py:54
  18.6 8.2 %student.5 = (bf16[256,384]{1,0:T(8,128)(2,1)S(1)}, bf16[256,384]{1,0:T(8,128)(2,1)S(1)}, bf16[256,384]{1,0:T(8,128)(2,1)S(1)}, bf16[256,384]{1,0:T(8,128)(2,1)S...) custom-call(bf16[256,384]{1,0:T(8,128)(2,1)S(1)} %get-tuple-element.37.cur_ref, ...), custom_call_target="tpu_custom_call" | custom-call | flops 10000000000 | bytes 786432 | tf_op jit(solution)/shard_map/student/pallas_call | solution.py:256
  26.7 2.3 %teacher.6 = (bf16[256,384]{1,0:T(8,128)(2,1)S(1)}, bf16[256,384]{1,0:T(8,128)(2,1)S(1)}) custom-call(s32[1]{0:T(128)} %bitcast.lead_ref, bf16[256,384]{1,0:T(8,128)(2,1)S(1)} %bitcast.44, bf16[256,384]{1,0:T(8,128)(2,1)S(1)} %get-tuple-element.39.relay_ref, bf16[2,3456,384]{2,1,0:T(8,128)(2,1)S(1)} %bitcast.39), custom_call_target="tpu_custom_call" | custom-call | flops 1358954496 | bytes 5308416 | tf_op jit(solution)/shard_map/teacher/pallas_call | solution.py:54
  29.0 8.3 %student.6 = (bf16[256,384]{1,0:T(8,128)(2,1)S(1)}, bf16[256,384]{1,0:T(8,128)(2,1)S(1)}, bf16[256,384]{1,0:T(8,128)(2,1)S(1)}, bf16[256,384]{1,0:T(8,128)(2,1)S...) custom-call(bf16[256,384]{1,0:T(8,128)(2,1)S(1)} %get-tuple-element.40.cur_ref, ...), custom_call_target="tpu_custom_call" | custom-call | flops 10000000000 | bytes 786432 | tf_op jit(solution)/shard_map/student/pallas_call | solution.py:256
  37.4 2.3 %teacher.7 = (bf16[256,384]{1,0:T(8,128)(2,1)S(1)}, bf16[256,384]{1,0:T(8,128)(2,1)S(1)}) custom-call(s32[1]{0:T(128)} %bitcast.lead_ref, bf16[256,384]{1,0:T(8,128)(2,1)S(1)} %bitcast.43, bf16[256,384]{1,0:T(8,128)(2,1)S(1)} %get-tuple-element.42.relay_ref, bf16[2,3456,384]{2,1,0:T(8,128)(2,1)S(1)} %bitcast.40), custom_call_target="tpu_custom_call" | custom-call | flops 1358954496 | bytes 5308416 | tf_op jit(solution)/shard_map/teacher/pallas_call | solution.py:54
  39.7 8.1 %student.7 = (bf16[256,384]{1,0:T(8,128)(2,1)S(1)}, bf16[256,384]{1,0:T(8,128)(2,1)S(1)}, bf16[256,384]{1,0:T(8,128)(2,1)S(1)}, bf16[256,384]{1,0:T(8,128)(2,1)S(1)}, f32[2,3,7,8,128]{4,3,2,1,0:T(8,128)S(1)}) custom-call(bf16[256,384]{1,0:T(8,128)(2,1)S(1)} %get-tuple-element.47.cur_ref, bf16[256,384]{1,0:T(8,128)(2,1)S(1)} %get-tuple-element.43.teach_ref, ...), custom_call_target="tpu_custom_call" | custom-call | flops 10000000000 | bytes 786432 | tf_op jit(solution)/shard_map/student/pallas_call | solution.py:256
  47.8 0.1 fusion.30
  47.8 0.1 copy.24
  48.0 0.6 %fusion.15 = f32[384,384]{0,1:T(8,128)S(1)} fusion(bf16[256,384]{1,0:T(8,128)(2,1)S(1)} %get-tuple-element.56, bf16[256,384]{1,0:T(8,128)(2,1)S(1)} %get-tuple-element.55, bf16[256,384]{1,0:T(8,128)(2,1)S(1)} %get-tuple-element.54, bf16[256,384]{1,0:T(8,128)(2,1)S(1)} %get-tuple-element.53, bf16[256,384]{1,0:T(8,128)(2,1)S(1)} %get-tuple-element.60, ...), kind=kOutput, calls=%fused_computation.18 | convolution fusion | flops 308281344 | bytes 2162688 | tf_op jit(solution)/shard_map/dot_general | solution.py:303
  48.6 0.6 %fusion = f32[384,384]{0,1:T(8,128)S(1)} fusion(bf16[256,384]{1,0:T(8,128)(2,1)S(1)} %get-tuple-element.48, bf16[256,384]{1,0:T(8,128)(2,1)S(1)} %get-tuple-element.46, bf16[256,384]{1,0:T(8,128)(2,1)S(1)} %get-tuple-element.45, bf16[256,384]{1,0:T(8,128)(2,1)S(1)} %get-tuple-element.44, bf16[256,384]{1,0:T(8,128)(2,1)S(1)} %get-tuple-element.52, ...), kind=kOutput, calls=%fused_computation.3 | convolution fusion | flops 308281344 | bytes 2162688 | tf_op jit(solution)/shard_map/dot_general | solution.py:303
  49.2 0.1 pad_maximum_fusion
  49.3 0.2 dynamic-slice_convert_fusion
  49.5 0.1 collective-permute-start
  49.6 0.7 %copy.22 = bf16[8,2,16,384]{3,2,1,0:T(8,128)(2,1)} copy(bf16[8,2,16,384]{3,0,1,2:T(8,128)(2,1)S(1)} %bitcast.46) | data formatting | bytes 393216 | tf_op jit(solution)/shard_map/transpose | solution.py:318
  50.3 1.1 %collective-permute-done = bf16[192,866]{0,1:T(8,128)(2,1)S(1)} collective-permute-done((bf16[192,866]{0,1:T(8,128)(2,1)S(1)}, bf16[192,866]{0,1:T(8,128)(2,1)S(1)}, u32[]{:S(2)}, u32[]{:S(2)}) %collective-permute-start) | collective-permute-done | bytes 332576 | tf_op jit(solution)/shard_map/ppermute | solution.py:315
  51.4 0.3 convert_add_fusion
  51.7 0.1 slice_bitcast_fusion.1
  51.8 0.1 pad_maximum_fusion.1
  51.8 1.1 %copy.25 = f32[2,384,192]{1,2,0:T(8,128)} copy(f32[2,384,192]{2,1,0:T(8,128)S(1)} %pad_maximum_fusion.1) | data formatting | bytes 1179648
  52.9 0.7 %copy.26 = f32[2,49,192]{2,0,1:T(2,128)} copy(f32[2,49,192]{2,1,0:T(8,128)S(1)} %reshape.43) | data formatting | bytes 150528
  (6 shorter events, 0.1 us)
Async XLA Ops:
  0.6 1.4 %copy-start.2 = (bf16[1,1,8,32,384]{4,3,2,1,0:T(8,128)(2,1)S(1)}, bf16[1,1,8,32,384]{4,3,2,1,0:T(8,128)(2,1)}, u32[]{:S(2)}) copy-start(bf16[1,1,8,32,384]{4,3,2,1,0:T(8,128)(2,1)} %param.5) | copy-start | bytes 589828
  0.6 1.5 %copy-start.3 = (f32[2,49,384]{2,0,1:T(2,128)S(1)}, f32[2,49,384]{2,0,1:T(2,128)}, u32[]{:S(2)}) copy-start(f32[2,49,384]{2,0,1:T(2,128)} %param.8) | copy-start | bytes 451588
  2.2 2.5 %copy-start = (bf16[2,3,3,384,384]{4,3,2,1,0:T(8,128)(2,1)S(1)}, bf16[2,3,3,384,384]{4,3,2,1,0:T(8,128)(2,1)}, u32[]{:S(2)}) copy-start(bf16[2,3,3,384,384]{4,3,2,1,0:T(8,128)(2,1)} %param.7) | copy-start | bytes 15925252
  4.7 2.4 %copy-start.1 = (bf16[2,384,384]{2,1,0:T(8,128)(2,1)S(1)}, bf16[2,384,384]{2,1,0:T(8,128)(2,1)}, u32[]{:S(2)}) copy-start(bf16[2,384,384]{2,1,0:T(8,128)(2,1)} %point_ref.7) | copy-start | bytes 1769476
  4.7 11.6 %slice-start = ((s8[5308416]{0:T(1024)(128)(4,1)}), s8[4194304]{0:T(1024)(128)(4,1)S(1)}, s32[]{:S(2)}) async-start(s8[5308416]{0:T(1024)(128)(4,1)} %bitcast.36), calls=%async_computation | async-start | bytes 8388608
  7.1 9.2 %slice-start.1 = ((s8[5308416]{0:T(1024)(128)(4,1)}), s8[1114112]{0:T(1024)(128)(4,1)S(1)}, s32[]{:S(2)}) async-start(s8[5308416]{0:T(1024)(128)(4,1)} %bitcast.36), calls=%async_computation.1 | async-start | bytes 2228224
  49.5 1.9 %collective-permute-start = (bf16[192,866]{0,1:T(8,128)(2,1)S(1)}, bf16[192,866]{0,1:T(8,128)(2,1)S(1)}, u32[]{:S(2)}, u32[]{:S(2)}) collective-permute-start(bf16[192,866]{0,1:T(8,128)(2,1)S(1)} %dynamic-slice_convert_fusion), channel_id=1, source_target_pairs={{0,1},{1,0},{2,3},{3,2},{4,5},{5,4},{6,7},{7,6},{8,9},{9,8},{10,11... | collective-permute-start | bytes 997640 | tf_op jit(solution)/shard_map/ppermute | solution.py:315

commit v4 on v3

--- a/solution.py
+++ b/solution.py
@@ -139,7 +139,7 @@
             device_id={"section": later},
             device_id_type=MESH,
         )
-    src0, src1, src2, slope0, slope1, dact, u_one_ref, resid_ref = rest
+    src0, src1, src2, slope0, slope1, dact, u_one_ref, resid_ref, sums_ref = rest
     gels, grads = (gel0, gel1), (grad0, grad1)
     rows, chans = cur_ref.shape
     blocks = chans // LANES
@@ -195,12 +195,14 @@
                 while size > 1:
                     size //= 2
                     prod = prod[:size] + prod[size:]
-                line = jnp.sum(prod[0].astype(F32), axis=0, keepdims=True)
-                dk_ref[which, block, row, col : col + 1, :] = line
-            dk_ref[which, block, row, 7:8, :] = jnp.zeros((1, LANES), F32)
+                wide = prod[0].astype(F32)
+                sums_ref[block, row, col] = wide[:height] + wide[height:]
             return carry
 
         lax.fori_loop(0, 7 * blocks, over_rows, 0)
+        for block in range(blocks):
+            for row in range(7):
+                dk_ref[which, block, row] = jnp.sum(sums_ref[block, row], axis=1)
 
     def back_point(which):
         dgel = lax.dot_general(grads[which][...], point_ref[which], NT, preferred_element_type=F32)
@@ -246,8 +248,8 @@
     spread_shape = pltpu.VMEM((blocks, 7, half + 6, 2 * height, LANES), F32)
     map_shape = pltpu.VMEM((rows, chans), F32)
     flat = jax.ShapeDtypeStruct((rows, chans), BF16)
-    outs = [flat] * 4 + [jax.ShapeDtypeStruct((2, blocks, 7, 8, LANES), F32)]
-    scratch = [spread_shape] * 3 + [map_shape] * 5
+    outs = [flat] * 4 + [jax.ShapeDtypeStruct((2, blocks, 7, 7, LANES), F32)]
+    scratch = [spread_shape] * 3 + [map_shape] * 5 + [pltpu.VMEM((blocks, 7, 7, height, LANES), F32)]
     params = {}
     if sections:
         outs.append(flat)
@@ -303,7 +305,7 @@
         lax.dot_general(grad_all[b], gel_all[b], (((0,), (0,)), ((), ())), preferred_element_type=F32)
         for b in range(2)
     ]
-    depth_rows = depth_total[:, :, :, :7].transpose(1, 4, 0, 2, 3).reshape(chans, 98)
+    depth_rows = depth_total.transpose(1, 4, 0, 2, 3).reshape(chans, 98)
     packed = jnp.concatenate(point_total + [depth_rows], axis=1)
     parties = lax.axis_size("dp")
     share = chans // parties
@@ -313,7 +315,7 @@
         out = lax.dynamic_slice_in_dim(packed, lax.rem(me + hop, parties) * share, share, 0)
         pairs = [(i, (i + hop) % parties) for i in range(parties)]
         total = total + lax.ppermute(out.astype(BF16), "dp", pairs).astype(F32)
-    point_grad = jnp.stack([total[:, b * chans : (b + 1) * chans].T for b in range(2)])
+    point_grad = jnp.stack([total[:, b * chans : (b + 1) * chans] for b in range(2)]).swapaxes(1, 2)
     depth_grad = total[:, 2 * chans :].T.reshape(2, 49, share)
     final = jnp.swapaxes(teach.reshape(width // 2, 2, height, chans), 0, 2)
     final = final.reshape(1, 1, height, width, chans)

time: 54.2 us -> 53.4 us (0.985)
  Pallas kernels: 43 us -> 41.9 us
    pallas_call x4, Pallas kernels: 33.7 us -> 32.6 us  [student(): pl.pallas_call(functools.partial(student_kernel, height, half // 2, secti...]
where the time goes in v4:
time: 53.4 us; the launch traced here: 52.5 us
  Pallas kernels  41.9 us (78%)
  local copies, waits for them, and re-layouts  6.82 us (13%)
  matrix products  1.24 us (2%)
  waiting for transfers between devices  1.07 us (2%)
  between operations  0.88 us (2%)
    pallas_call x4, Pallas kernels, student(): pl.pallas_call(functools.partial(student_kernel, height, half // 2, secti...  32.6 us
    pallas_call x4, Pallas kernels, teacher(): pl.pallas_call(functools.partial(teacher_kernel, height), out_shape=(jax....  9.32 us
    unnamed x17, local copies, waits for them, and re-layouts  4.35 us
    another operation x2, local copies, waits for them, and re-layouts, to_rows(): split = maps.reshape(front + (height, 2, width // 2, chans))  1.37 us
    dot_general x2, matrix products, body(): lax.dot_general(grad_all[b], gel_all[b], (((0,), (0,)), ((), ())), prefer...  1.24 us
    ppermute x1, waiting for transfers between devices, body(): total = total + lax.ppermute(out.astype(BF16), 'dp', pairs).astype(F32)  1.07 us
  transfers between devices with their start and end apart: 1, of which 1 were waited for; matrix products, arithmetic and copies ran while one was open for 1% of the time, Pallas kernels for 0%

profile of v4, /device:TPU:0, one launch (start us, length us, event | category | flops | bytes accessed | tf_op | source)
XLA Modules:
  0.0 52.5 jit_solution(14485634176596887140)
XLA Ops:
  0.6 0.0 copy-start.2
  0.6 0.0 copy-start.3
  0.7 1.3 %copy.29 = bf16[3,8,2,16,384]{4,1,2,3,0:T(8,128)(2,1)S(1)} copy(bf16[3,8,2,16,384]{4,3,2,1,0:T(8,128)(2,1)} %bitcast.49) | data formatting | bytes 1179648 | tf_op jit(solution)/shard_map/reshape;squeeze | solution.py:281
  2.0 0.1 fusion.32
  2.0 0.0 copy-done.2
  2.0 0.1 copy.18
  2.1 0.0 copy-done.3
  2.2 0.0 copy-start
  2.2 2.5 %copy-done = bf16[2,3,3,384,384]{4,3,2,1,0:T(8,128)(2,1)S(1)} copy-done((bf16[2,3,3,384,384]{4,3,2,1,0:T(8,128)(2,1)S(1)}, bf16[2,3,3,384,384]{4,3,2,1,0:T(8,128)(2,1)}, u32[]{:S(2)}) %copy-start) | copy-done | bytes 5308440
  4.7 0.0 copy-start.1
  4.7 0.0 slice-start
  4.7 2.4 %teacher.4 = (bf16[256,384]{1,0:T(8,128)(2,1)S(1)}, bf16[256,384]{1,0:T(8,128)(2,1)S(1)}) custom-call(s32[1]{0:T(128)} %bitcast.lead_ref, bf16[256,384]{1,0:T(8,128)(2,1)S(1)} %bitcast.39, bf16[256,384]{1,0:T(8,128)(2,1)S(1)} %bitcast.40, bf16[2,3456,384]{2,1,0:T(8,128)(2,1)S(1)} %bitcast.33), custom_call_target="tpu_custom_call" | custom-call | flops 1358954496 | bytes 5308416 | tf_op jit(solution)/shard_map/teacher/pallas_call | solution.py:54
  7.0 0.0 copy-done.1
  7.1 0.0 slice-start.1
  7.1 8.9 %student.4 = (bf16[256,384]{1,0:T(8,128)(2,1)S(1)}, bf16[256,384]{1,0:T(8,128)(2,1)S(1)}, bf16[256,384]{1,0:T(8,128)(2,1)S(1)}, bf16[256,384]{1,0:T(8,128)(2,1)S...) custom-call(bf16[256,384]{1,0:T(8,128)(2,1)S(1)} %get-tuple-element.34.cur_ref, ...), custom_call_target="tpu_custom_call" | custom-call | flops 10000000000 | bytes 786432 | tf_op jit(solution)/shard_map/student/pallas_call | solution.py:258
  15.9 0.0 slice-done
  16.0 0.0 slice-done.1
  16.0 2.3 %teacher.5 = (bf16[256,384]{1,0:T(8,128)(2,1)S(1)}, bf16[256,384]{1,0:T(8,128)(2,1)S(1)}) custom-call(s32[1]{0:T(128)} %bitcast.lead_ref, bf16[256,384]{1,0:T(8,128)(2,1)S(1)} %bitcast.43, bf16[256,384]{1,0:T(8,128)(2,1)S(1)} %get-tuple-element.36.relay_ref, bf16[2,3456,384]{2,1,0:T(8,128)(2,1)S(1)} %bitcast.36), custom_call_target="tpu_custom_call" | custom-call | flops 1358954496 | bytes 5308416 | tf_op jit(solution)/shard_map/teacher/pallas_call | solution.py:54
  18.3 7.9 %student.5 = (bf16[256,384]{1,0:T(8,128)(2,1)S(1)}, bf16[256,384]{1,0:T(8,128)(2,1)S(1)}, bf16[256,384]{1,0:T(8,128)(2,1)S(1)}, bf16[256,384]{1,0:T(8,128)(2,1)S...) custom-call(bf16[256,384]{1,0:T(8,128)(2,1)S(1)} %get-tuple-element.37.cur_ref, ...), custom_call_target="tpu_custom_call" | custom-call | flops 10000000000 | bytes 786432 | tf_op jit(solution)/shard_map/student/pallas_call | solution.py:258
  26.2 2.3 %teacher.6 = (bf16[256,384]{1,0:T(8,128)(2,1)S(1)}, bf16[256,384]{1,0:T(8,128)(2,1)S(1)}) custom-call(s32[1]{0:T(128)} %bitcast.lead_ref, bf16[256,384]{1,0:T(8,128)(2,1)S(1)} %bitcast.42, bf16[256,384]{1,0:T(8,128)(2,1)S(1)} %get-tuple-element.39.relay_ref, bf16[2,3456,384]{2,1,0:T(8,128)(2,1)S(1)} %bitcast.37), custom_call_target="tpu_custom_call" | custom-call | flops 1358954496 | bytes 5308416 | tf_op jit(solution)/shard_map/teacher/pallas_call | solution.py:54
  28.5 8.1 %student.6 = (bf16[256,384]{1,0:T(8,128)(2,1)S(1)}, bf16[256,384]{1,0:T(8,128)(2,1)S(1)}, bf16[256,384]{1,0:T(8,128)(2,1)S(1)}, bf16[256,384]{1,0:T(8,128)(2,1)S...) custom-call(bf16[256,384]{1,0:T(8,128)(2,1)S(1)} %get-tuple-element.40.cur_ref, ...), custom_call_target="tpu_custom_call" | custom-call | flops 10000000000 | bytes 786432 | tf_op jit(solution)/shard_map/student/pallas_call | solution.py:258
  36.5 2.3 %teacher.7 = (bf16[256,384]{1,0:T(8,128)(2,1)S(1)}, bf16[256,384]{1,0:T(8,128)(2,1)S(1)}) custom-call(s32[1]{0:T(128)} %bitcast.lead_ref, bf16[256,384]{1,0:T(8,128)(2,1)S(1)} %bitcast.41, bf16[256,384]{1,0:T(8,128)(2,1)S(1)} %get-tuple-element.42.relay_ref, bf16[2,3456,384]{2,1,0:T(8,128)(2,1)S(1)} %bitcast.38), custom_call_target="tpu_custom_call" | custom-call | flops 1358954496 | bytes 5308416 | tf_op jit(solution)/shard_map/teacher/pallas_call | solution.py:54
  38.9 7.8 %student.7 = (bf16[256,384]{1,0:T(8,128)(2,1)S(1)}, bf16[256,384]{1,0:T(8,128)(2,1)S(1)}, bf16[256,384]{1,0:T(8,128)(2,1)S(1)}, bf16[256,384]{1,0:T(8,128)(2,1)S(1)}, f32[2,3,7,7,128]{4,3,2,1,0:T(8,128)S(1)}) custom-call(bf16[256,384]{1,0:T(8,128)(2,1)S(1)} %get-tuple-element.47.cur_ref, bf16[256,384]{1,0:T(8,128)(2,1)S(1)} %get-tuple-element.43.teach_ref, ...), custom_call_target="tpu_custom_call" | custom-call | flops 10000000000 | bytes 786432 | tf_op jit(solution)/shard_map/student/pallas_call | solution.py:258
  46.7 0.1 add_bitcast_fusion
  46.7 0.1 copy.24
  46.9 0.6 %fusion.15 = f32[384,384]{0,1:T(8,128)S(1)} fusion(bf16[256,384]{1,0:T(8,128)(2,1)S(1)} %get-tuple-element.56, bf16[256,384]{1,0:T(8,128)(2,1)S(1)} %get-tuple-element.55, bf16[256,384]{1,0:T(8,128)(2,1)S(1)} %get-tuple-element.54, bf16[256,384]{1,0:T(8,128)(2,1)S(1)} %get-tuple-element.53, bf16[256,384]{1,0:T(8,128)(2,1)S(1)} %get-tuple-element.60, ...), kind=kOutput, calls=%fused_computation.18 | convolution fusion | flops 308281344 | bytes 2162688 | tf_op jit(solution)/shard_map/dot_general | solution.py:305
  47.5 0.6 %fusion = f32[384,384]{0,1:T(8,128)S(1)} fusion(bf16[256,384]{1,0:T(8,128)(2,1)S(1)} %get-tuple-element.48, bf16[256,384]{1,0:T(8,128)(2,1)S(1)} %get-tuple-element.46, bf16[256,384]{1,0:T(8,128)(2,1)S(1)} %get-tuple-element.45, bf16[256,384]{1,0:T(8,128)(2,1)S(1)} %get-tuple-element.44, bf16[256,384]{1,0:T(8,128)(2,1)S(1)} %get-tuple-element.52, ...), kind=kOutput, calls=%fused_computation.3 | convolution fusion | flops 308281344 | bytes 2162688 | tf_op jit(solution)/shard_map/dot_general | solution.py:305
  48.1 0.1 pad_maximum_fusion
  48.2 0.2 dynamic-slice_convert_fusion
  48.4 0.1 collective-permute-start
  48.5 0.7 %copy.22 = bf16[8,2,16,384]{3,2,1,0:T(8,128)(2,1)} copy(bf16[8,2,16,384]{3,0,1,2:T(8,128)(2,1)S(1)} %bitcast.44) | data formatting | bytes 393216 | tf_op jit(solution)/shard_map/transpose | solution.py:320
  49.2 1.1 %collective-permute-done = bf16[192,866]{0,1:T(8,128)(2,1)S(1)} collective-permute-done((bf16[192,866]{0,1:T(8,128)(2,1)S(1)}, bf16[192,866]{0,1:T(8,128)(2,1)S(1)}, u32[]{:S(2)}, u32[]{:S(2)}) %collective-permute-start) | collective-permute-done | bytes 332576 | tf_op jit(solution)/shard_map/ppermute | solution.py:317
  50.3 0.3 convert_add_fusion
  50.6 0.1 slice_bitcast_fusion.1
  50.7 0.1 maximum_bitcast_fusion
  50.8 1.1 %copy.25 = f32[2,384,192]{1,2,0:T(8,128)} copy(f32[2,384,192]{2,1,0:T(8,128)S(1)} %maximum_bitcast_fusion) | data formatting | bytes 1179648
  51.8 0.7 %copy.26 = f32[2,49,192]{2,0,1:T(2,128)} copy(f32[2,49,192]{2,1,0:T(8,128)S(1)} %reshape.43) | data formatting | bytes 150528
  (6 shorter events, 0.1 us)
Async XLA Ops:
  0.6 1.4 %copy-start.2 = (bf16[1,1,8,32,384]{4,3,2,1,0:T(8,128)(2,1)S(1)}, bf16[1,1,8,32,384]{4,3,2,1,0:T(8,128)(2,1)}, u32[]{:S(2)}) copy-start(bf16[1,1,8,32,384]{4,3,2,1,0:T(8,128)(2,1)} %param.5) | copy-start | bytes 589828
  0.6 1.5 %copy-start.3 = (f32[2,49,384]{2,0,1:T(2,128)S(1)}, f32[2,49,384]{2,0,1:T(2,128)}, u32[]{:S(2)}) copy-start(f32[2,49,384]{2,0,1:T(2,128)} %param.8) | copy-start | bytes 451588
  2.2 2.5 %copy-start = (bf16[2,3,3,384,384]{4,3,2,1,0:T(8,128)(2,1)S(1)}, bf16[2,3,3,384,384]{4,3,2,1,0:T(8,128)(2,1)}, u32[]{:S(2)}) copy-start(bf16[2,3,3,384,384]{4,3,2,1,0:T(8,128)(2,1)} %param.7) | copy-start | bytes 15925252
  4.7 2.4 %copy-start.1 = (bf16[2,384,384]{2,1,0:T(8,128)(2,1)S(1)}, bf16[2,384,384]{2,1,0:T(8,128)(2,1)}, u32[]{:S(2)}) copy-start(bf16[2,384,384]{2,1,0:T(8,128)(2,1)} %point_ref.7) | copy-start | bytes 1769476
  4.7 11.3 %slice-start = ((s8[5308416]{0:T(1024)(128)(4,1)}), s8[4194304]{0:T(1024)(128)(4,1)S(1)}, s32[]{:S(2)}) async-start(s8[5308416]{0:T(1024)(128)(4,1)} %bitcast.34), calls=%async_computation | async-start | bytes 8388608
  7.1 8.9 %slice-start.1 = ((s8[5308416]{0:T(1024)(128)(4,1)}), s8[1114112]{0:T(1024)(128)(4,1)S(1)}, s32[]{:S(2)}) async-start(s8[5308416]{0:T(1024)(128)(4,1)} %bitcast.34), calls=%async_computation.1 | async-start | bytes 2228224
  48.4 1.9 %collective-permute-start = (bf16[192,866]{0,1:T(8,128)(2,1)S(1)}, bf16[192,866]{0,1:T(8,128)(2,1)S(1)}, u32[]{:S(2)}, u32[]{:S(2)}) collective-permute-start(bf16[192,866]{0,1:T(8,128)(2,1)S(1)} %dynamic-slice_convert_fusion), channel_id=1, source_target_pairs={{0,1},{1,0},{2,3},{3,2},{4,5},{5,4},{6,7},{7,6},{8,9},{9,8},{10,11... | collective-permute-start | bytes 997640 | tf_op jit(solution)/shard_map/ppermute | solution.py:317
